TPU v7x, 128 devices: a whole 4x4x4 slice. The times are simulated.
128 devices in a mesh: dp: 64 (over y, x_lo, z, core), tensor: 2 (over x_hi).
Axes of the slice: x: 4 (x_hi: 2, x_lo: 2; x = x_hi * 2 + x_lo), y: 4, z: 4, core: 2. Of those that a mesh axis runs over, the one named last changes fastest.
Arguments:
- tokens: bfloat16 [64, 512, 896], P(None, 'dp'), may hold values from -6 to 6
- cotangent: bfloat16 [64, 512, 896], P(None, 'dp'), may hold values from -6 to 6
- lengths: int32 [64], replicated, may hold values from 1 to 512, 24576 in all
- deal_order: int32 [64], replicated, may hold values from 0 to 63, each once
- gain_attn: bfloat16 [896], replicated, may hold values from 0.099609375 to 1.8984375
- w_query: bfloat16 [896, 896], P(None, 'tensor'), may hold values from -0.1875 to 0.1875
- b_query: bfloat16 [896], P('tensor'), may hold values from -3 to 3
- w_key: bfloat16 [896, 128], P(None, 'tensor'), may hold values from -0.1875 to 0.1875
- b_key: bfloat16 [128], P('tensor'), may hold values from -3 to 3
- w_value: bfloat16 [896, 128], P(None, 'tensor'), may hold values from -0.1875 to 0.1875
- b_value: bfloat16 [128], P('tensor'), may hold values from -3 to 3
- w_out: bfloat16 [896, 896], P('tensor'), may hold values from -1 to 1
- gain_mlp: bfloat16 [896], replicated, may hold values from 0.099609375 to 1.8984375
- w_gate: bfloat16 [896, 4864], P(None, 'tensor'), may hold values from -0.1875 to 0.1875
- w_up: bfloat16 [896, 4864], P(None, 'tensor'), may hold values from -0.1875 to 0.1875
- w_down: bfloat16 [4864, 896], P('tensor'), may hold values from -0.078125 to 0.078125
Outputs:
- layer_out: bfloat16 [64, 512, 896], P(None, 'dp')
- grad_tokens: bfloat16 [64, 512, 896], P(None, 'dp')
- grad_gain_attn: float32 [896], replicated
- grad_w_query: float32 [896, 896], P(None, 'tensor')
- grad_b_query: float32 [896], P('tensor')
- grad_w_key: float32 [896, 128], P(None, 'tensor')
- grad_b_key: float32 [128], P('tensor')
- grad_w_value: float32 [896, 128], P(None, 'tensor')
- grad_b_value: float32 [128], P('tensor')
- grad_w_out: float32 [896, 896], P('tensor')
- grad_gain_mlp: float32 [896], replicated
- grad_w_gate: float32 [896, 4864], P(None, 'tensor')
- grad_w_up: float32 [896, 4864], P(None, 'tensor')
- grad_w_down: float32 [4864, 896], P('tensor')
- rms_values: float32 [3], replicated
Inputs may be any that keep to these rules, and one draw needn't show every extreme that they name: Group g receives stored slot deal_order[g]; every slot goes to exactly one group. The first lengths[g] rows of the slot that group g receives are valid.
All inputs are finite; a program needn't handle non-finite values.
Results may differ from a plain program's by a relative error of at most 0.022.
Values may be sent and summed in bfloat16 or wider, within the bound.
A program may use at most 192 MiB of HBM per device.

v0:
```python
import functools
import math

import jax
import jax.numpy as jnp
import numpy as np
from jax import lax
from jax.experimental import pallas as pl
from jax.experimental.pallas import tpu as pltpu
from jax.sharding import PartitionSpec as P

MESH = pl.DeviceIdType.MESH
HD = 64
epsilon = 1e-06
rope_base = 1000000.0
VMEM_LIMIT = 60 << 20
LINKS = ("x", "ya", "za", "yb", "zb")


def flip(dp):
    return dp + 8 - 16 * ((dp // 8) % 2)


def group_of(dp, t):
    return dp + t * (flip(dp) - dp)


def coords():
    return lax.axis_index("dp"), lax.axis_index("tensor")


def partner(dim, dp, t):
    y, xl, z, c = dp // 16, (dp // 8) % 2, (dp // 2) % 4, dp % 2
    if dim == "core":
        c = 1 - c
    if dim == "x":
        xl = 1 - xl
    if dim == "ya":
        y = y + 1 - 2 * (y % 2)
    if dim == "yb":
        y = 3 - y
    if dim == "za":
        z = z + 1 - 2 * (z % 2)
    if dim == "zb":
        z = 3 - z
    if dim == "tn":
        xl, t = 1 - xl, 1 - t
    return (((y * 2 + xl) * 4 + z) * 2 + c, t)


def bit(dim, dp):
    y, xl, z, c = dp // 16, (dp // 8) % 2, (dp // 2) % 4, dp % 2
    return {
        "core": c,
        "x": xl,
        "ya": ((y + 1) // 2) % 2,
        "yb": y // 2,
        "za": ((z + 1) // 2) % 2,
        "zb": z // 2,
    }[dim]


def greet(partners):
    barrier = pltpu.get_barrier_semaphore()
    for who in partners:
        pl.semaphore_signal(barrier, inc=1, device_id=who, device_id_type=MESH)


def around(dp, t, axis, j):
    a, b = dp // 8, dp % 8
    return (((a + j) % 8 * 8 + b) if axis == 0 else a * 8 + (b + j) % 8, t)


def neighbours(dp, t):
    return [around(dp, t, axis, j) for axis in range(2) for j in range(1, 8)]


def met(n):
    pl.semaphore_wait(pltpu.get_barrier_semaphore(), n)


def remote(src, dst, send, recv, who):
    return pltpu.make_async_remote_copy(
        src_ref=src, dst_ref=dst, send_sem=send, recv_sem=recv, device_id=who, device_id_type=MESH
    )


def put_sum(dst, src, row, lane, other, rows, lanes):
    step = 16
    while step * 2 * lanes <= 32768 and rows % (step * 2) == 0:
        step *= 2

    def body(i, carry):
        here = pl.ds(pl.multiple_of(i * step, 16), step)
        there = pl.ds(pl.multiple_of(row + i * step, 16), step)
        lane_at = lane if isinstance(lane, int) else pl.multiple_of(lane, 128)
        dst[here, :] = src[there, pl.ds(lane_at, lanes)] + other[here, :]
        return carry

    lax.fori_loop(0, rows // step, body, 0)


def halves(rows, lanes, kinds):
    out = []
    for kind in kinds:
        if kind == "r":
            rows //= 2
        elif kind == "l":
            lanes //= 2
        out.append((rows, lanes))
    return out


class Chain:
    def __init__(self, rows, lanes, kinds, turn, dp, t):
        self.kinds = kinds
        self.dims = ("core",) + tuple(LINKS[(turn + i) % 5] for i in range(5))
        self.who = [partner(d, dp, t) for d in self.dims]
        self.bits = [bit(d, dp) for d in self.dims]
        self.shapes = [(rows, lanes)] + halves(rows, lanes, kinds)
        self.last = max(i for i, kind in enumerate(kinds) if kind != "f")
        self.corner = [(0, 0)]
        for s, kind in enumerate(kinds):
            row, lane = self.corner[-1]
            rows, lanes = self.shapes[s + 1]
            b = self.bits[s]
            self.corner.append((row + (b * rows if kind == "r" else 0), lane + (b * lanes if kind == "l" else 0)))

    def start(self, s, src, got, send, recv):
        rows, lanes = self.shapes[s + 1]
        give, self.keep = (0, 0), (0, 0)
        b = self.bits[s]
        if self.kinds[s] == "r":
            give, self.keep = (pl.multiple_of((1 - b) * rows, 16), 0), (b * rows, 0)
        elif self.kinds[s] == "l":
            give, self.keep = (0, pl.multiple_of((1 - b) * lanes, 128)), (0, b * lanes)
        self.src, self.got = src, got
        self.copy = remote(src.at[pl.ds(give[0], rows), pl.ds(give[1], lanes)], got, send, recv, self.who[s])
        self.copy.start()

    def finish(self, s, dst):
        self.copy.wait()
        rows, lanes = self.shapes[s + 1]
        put_sum(dst, self.src, self.keep[0], self.keep[1], self.got, rows, lanes)

    def spot(self, s, full, base):
        rows, lanes = self.shapes[s]
        row, lane = self.corner[s]
        row, lane = row + base[0], lane + base[1]
        row = row if isinstance(row, int) else pl.multiple_of(row, 16)
        lane = lane if isinstance(lane, int) else pl.multiple_of(lane, 128)
        return full.at[pl.ds(row, rows), pl.ds(lane, lanes)]

    def gather_start(self, s, full, base, send, recv):
        mine = self.spot(s + 1, full, base)
        self.copy = remote(mine, mine, send, recv, self.who[s])
        self.copy.start()

    def gather_finish(self):
        self.copy.wait()


G_KINDS = ("l", "l", "r", "r", "r", "f")
D_KINDS = ("r", "r", "r", "r", "r", "f")
K_KINDS = ("r", "r", "r", "f", "f", "f")
ANY_SPEC = pl.BlockSpec(memory_space=pl.ANY)
G_SHAPES = halves(896, 512, G_KINDS)
D_SHAPES = halves(512, 896, D_KINDS)
K_SHAPES = halves(128, 896, K_KINDS)
BF, F32 = jnp.bfloat16, jnp.float32
VMEM_SPEC = pl.BlockSpec(memory_space=pltpu.VMEM)
SMEM_SPEC = pl.BlockSpec(memory_space=pltpu.SMEM)
BLOCK = jax.ShapeDtypeStruct((64, 8, 896), BF)
DMA = pltpu.SemaphoreType.DMA


def params(cid):
    return pltpu.CompilerParams(collective_id=cid, has_side_effects=True, vmem_limit_bytes=VMEM_LIMIT)


class Mail:
    LOW = 512

    def __init__(self, buf, mids, out, spot, send, recv, dp, t):
        self.buf, self.mids, self.out = buf, mids, out
        self.me = (dp // 8, dp % 8)
        self.spot = spot
        self.send, self.recv, self.dp, self.t = send, recv, dp, t
        self.lanes = (pl.ds(0, self.LOW), pl.ds(self.LOW, 896 - self.LOW))

    def first(self):
        self.copies = [[], []]
        for j in range(1, 8):
            for f in range(2):
                to = (self.me[f] + j) % 8
                src = self.buf.at[to, :, :, self.lanes[f]] if f == 0 else self.buf.at[:, to, :, self.lanes[f]]
                c = remote(src, self.mids[f].at[self.spot[f]], self.send.at[0, f, j], self.recv.at[0, f, j],
                           around(self.dp, self.t, f, j))
                c.start()
                self.copies[f].append(c)
        for f in range(2):
            me = self.me[f]
            own = self.buf[me, :, :, self.lanes[f]] if f == 0 else self.buf[:, me, :, self.lanes[f]]
            self.mids[f][self.spot[f]] = own

    def second(self):
        for f in range(2):
            for c in self.copies[f]:
                c.wait()
        self.copies = []
        for j in range(1, 8):
            for f in range(2):
                g = 1 - f
                to = (self.me[g] + j) % 8
                dst = self.out.at[:, self.spot[1], :, self.lanes[f]] if f == 0 else self.out.at[self.spot[0], :, :, self.lanes[f]]
                c = remote(self.mids[f].at[:, to], dst, self.send.at[1, f, j], self.recv.at[1, f, j],
                           around(self.dp, self.t, g, j))
                c.start()
                self.copies.append(c)
        for f in range(2):
            own = self.mids[f][:, self.me[1 - f]]
            if f == 0:
                self.out[:, self.spot[1], :, self.lanes[f]] = own
            else:
                self.out[self.spot[0], :, :, self.lanes[f]] = own

    def last(self):
        for c in self.copies:
            c.wait()


MAIL = jax.ShapeDtypeStruct((8, 8, 8, 896), BF)
MAIL_SCRATCH = [
    pltpu.VMEM((8, 8, 8, 896), BF), pltpu.VMEM((8, 8, 8, 512), BF), pltpu.VMEM((8, 8, 8, 384), BF),
    DMA((2, 2, 8)), DMA((2, 2, 8)),
]


def sort_out(order, rows, buf, dp, t):
    for a in range(8):
        for b in range(8):
            buf[a, b] = rows[order[group_of(a * 8 + b, t)]]


def dispatch_kernel(order, tok, out, buf, mid0, mid1, send, recv):
    dp, t = coords()
    greet(neighbours(dp, t))
    sort_out(order, tok, buf, dp, t)
    mail = Mail(buf, (mid0, mid1), out, (dp // 8, dp % 8), send, recv, dp, t)
    met(14)
    mail.first()
    mail.second()
    mail.last()


def dispatch(order, tokens):
    return pl.pallas_call(
        dispatch_kernel,
        out_shape=MAIL,
        in_specs=[SMEM_SPEC, VMEM_SPEC],
        out_specs=VMEM_SPEC,
        scratch_shapes=MAIL_SCRATCH,
        compiler_params=params(1),
        name="dispatch",
    )(order, tokens)


def mm(a, b):
    return jnp.dot(a, b, preferred_element_type=F32)


def mm_t(a, b):
    return lax.dot_general(a, b, (((1,), (1,)), ((), ())), preferred_element_type=F32)


def t_mm(a, b):
    return lax.dot_general(a, b, (((0,), (0,)), ((), ())), preferred_element_type=F32)


def rope_table():
    places = np.arange(512, dtype=np.float32)
    frequency = np.power(np.float32(rope_base), -np.arange(32, dtype=np.float32) * np.float32(2.0 / HD)).astype(np.float32)
    angles = (places[:, None] * frequency[None, :]).astype(np.float64)
    cos, sin = np.cos(angles), np.sin(angles)
    return np.concatenate([cos, cos, sin, sin], axis=1).astype(np.float32)


def first_half(shape):
    return lax.broadcasted_iota(jnp.int32, shape, 1) % 64 < 32


def spread(table):
    other = pltpu.roll(table, 64, 1)
    low = lax.broadcasted_iota(jnp.int32, table.shape, 1) < 64
    cos, sin = jnp.where(low, table, other), jnp.where(low, other, table)
    return cos, jnp.where(first_half(table.shape), -sin, sin)


def turn(x, cos, sin):
    swapped = jnp.where(first_half(x.shape), pltpu.roll(x, 96, 1), pltpu.roll(x, 32, 1))
    return x * cos + swapped * sin


def one_head(pair, side):
    low = lax.broadcasted_iota(jnp.int32, pair.shape, 1) < 64
    return jnp.where(low if side == 0 else jnp.logical_not(low), pair, jnp.zeros_like(pair))


def fill_mask(mask, length):
    for b in range(2):
        rows = lax.broadcasted_iota(jnp.int32, (256, 512), 0) + b * 256
        cols = lax.broadcasted_iota(jnp.int32, (256, 512), 1)
        mask[pl.ds(b * 256, 256), :] = jnp.where((cols <= rows) & (cols < length), 0.0, -1e30)


class Swap:
    def __init__(self, x, got, send, recv, dp, t):
        self.who = partner("tn", dp, t)
        self.x, self.got, self.send, self.recv = x, got, send, recv
        self.copies = [None] * 4

    def start(self, i):
        rows = pl.ds(i * 128, 128)
        self.copies[i] = remote(self.x.at[rows], self.got.at[rows], self.send.at[i], self.recv.at[i], self.who)
        self.copies[i].start()

    def take(self, i):
        self.copies[i].wait()
        rows = pl.ds(i * 128, 128)
        return self.x[rows, :].astype(F32) + self.got[rows, :].astype(F32)


def meet_kernel(
    order, lengths, stream, cot, wq, wk, wv, wo, vecs, table,
    normed, q_o, k_o, v_o, lse_o, mixed, residual, normed_two, gy, squares,
    sides, mask, x, got, cot_in, send, recv, buf, mid0, mid1, c_send, c_recv,
):
    dp, t = coords()
    swap = Swap(x, got, send, recv, dp, t)
    mail = Mail(buf, (mid0, mid1), cot_in, (dp // 8, dp % 8), c_send, c_recv, dp, t)
    greet(neighbours(dp, t) + [swap.who])
    length = lengths[group_of(dp, t)]
    sort_out(order, cot, buf, dp, t)
    for i in range(4):
        at = pl.ds(i * 128, 128)
        row = stream[at, :].astype(F32)
        inverse = lax.rsqrt(jnp.mean(row * row, axis=-1, keepdims=True) + epsilon)
        normed[at, :] = (row * inverse * vecs[0:1, :]).astype(BF)
    fill_mask(mask, length)
    cos, sin = spread(table[...])
    k = mm_t(normed[...], wk[...]) + vecs[2:3, 448:512]
    v = mm_t(normed[...], wv[...]) + vecs[2:3, 512:576]
    k2 = turn(jnp.concatenate([k, k], axis=1), cos, sin)
    k_o[...] = (k2.astype(BF).astype(F32) * 0.125).astype(BF)
    v_o[...] = jnp.concatenate([v, v], axis=1).astype(BF)
    for side in range(2):
        sides[side] = one_head(k_o[...], side)
        sides[2 + side] = one_head(v_o[...], side)
    met(15)
    mail.first()
    for p in range(4):
        w = 128 if p < 3 else 64
        lanes = pl.ds(128 * p, w)
        q = mm_t(normed[...], wq[lanes, :]) + vecs[2:3, lanes]
        if w < 128:
            q = jnp.concatenate([q, jnp.zeros((512, 64), F32)], axis=1)
        q_o[:, pl.ds(128 * p, 128)] = turn(q, cos, sin).astype(BF)
    for b in range(2):
        rows, keys = pl.ds(256 * b, 256), pl.ds(0, 256 * (b + 1))
        lse_o[rows, :] = jnp.zeros((256, 128), F32)

        def heads(p, both):
            lanes = pl.ds(pl.multiple_of(128 * p, 128), 128)
            pair = q_o[rows, lanes]
            total = jnp.zeros((256, 128), F32)
            for side in range(2 if both else 1):
                score = mm_t(pair, sides[side, keys, :]) + mask[rows, keys]
                top = jnp.max(score, axis=-1, keepdims=True)
                expo = jnp.exp(score - top)
                mass = jnp.sum(expo, axis=-1, keepdims=True)
                probs = (expo * (1.0 / mass)).astype(BF)
                total = total + mm(probs, sides[2 + side, keys, :])
                here = lax.broadcasted_iota(jnp.int32, (256, 128), 1) == 2 * p + side
                lse_o[rows, :] = jnp.where(here, top + jnp.log(mass), lse_o[rows, :])
            mixed[rows, lanes] = total.astype(BF)

        def body(p, carry):
            heads(p, True)
            return carry

        lax.fori_loop(0, 3, body, 0)
        heads(3, False)
        x[rows, :] = mm(mixed[rows, pl.ds(0, 448)], wo[...]).astype(BF)
        swap.start(2 * b)
        swap.start(2 * b + 1)
        if b == 0:
            mail.second()
    total = jnp.zeros((8, 896), F32)
    for i in range(4):
        at = pl.ds(i * 128, 128)
        valid = lax.broadcasted_iota(jnp.int32, (128, 896), 0) + i * 128 < length
        attention = swap.take(i)
        res = stream[at, :].astype(F32) + attention
        residual[at, :] = res
        inverse = lax.rsqrt(jnp.mean(res * res, axis=-1, keepdims=True) + epsilon)
        normed_two[at, :] = (res * inverse * vecs[1:2, :]).astype(BF)
        kept = jnp.where(valid, attention, 0.0)
        total = total + jnp.sum((kept * kept).reshape(16, 8, 896), axis=0)
    squares[...] = total
    mail.last()
    for i in range(4):
        at = pl.ds(i * 128, 128)
        valid = lax.broadcasted_iota(jnp.int32, (128, 896), 0) + i * 128 < length
        gy[at, :] = jnp.where(valid, cot_in[pl.ds(i * 2, 2)].astype(F32).reshape(128, 896), 0.0).astype(BF)


def meet(*operands):
    rows = jax.ShapeDtypeStruct((512, 896), BF)
    wide_rows = jax.ShapeDtypeStruct((512, 512), BF)
    pair = jax.ShapeDtypeStruct((512, 128), BF)
    return pl.pallas_call(
        meet_kernel,
        out_shape=(
            rows, wide_rows, pair, pair, jax.ShapeDtypeStruct((512, 128), F32), wide_rows,
            jax.ShapeDtypeStruct((512, 896), F32), rows, rows, jax.ShapeDtypeStruct((8, 896), F32),
        ),
        in_specs=[SMEM_SPEC] * 2 + [VMEM_SPEC] * 8,
        out_specs=(VMEM_SPEC,) * 10,
        scratch_shapes=[
            pltpu.VMEM((4, 512, 128), BF),
            pltpu.VMEM((512, 512), F32),
            pltpu.VMEM((512, 896), BF),
            pltpu.VMEM((512, 896), BF),
            pltpu.VMEM((8, 8, 8, 896), BF),
            DMA((4,)), DMA((4,)), *MAIL_SCRATCH,
        ],
        compiler_params=params(2),
        name="meet",
    )(*operands)


MORE = {10: 0, 11: 0, 12: 1, 13: 2, 14: 1}


def tile(p):
    return pl.ds(512 * p, 512 if p < 4 else 384)


def wide_kernel(
    normed, gy, w_gate, w_up, w_down, gn_out, mlp_out, g_out, d_out, g_more, d_more,
    gn_total, mlp_total, gn, got, hid, gg, gu, gate_w, up_w, down_w, g_src, d_src, g0, d0, g1, d1,
    x_send, x_recv, send, recv, local,
):
    dp, t = coords()
    swap = Swap(gn, got, x_send, x_recv, dp, t)
    greet([swap.who] + [partner(d, dp, t) for d in ("core",) + LINKS])
    loads = []

    def load(p):
        at, w = tile(p), 512 if p < 4 else 384
        b = p % 2
        copies = [
            pltpu.make_async_copy(w_gate.at[:, at], gate_w.at[b, :, pl.ds(0, w)], local.at[p, 0]),
            pltpu.make_async_copy(w_up.at[:, at], up_w.at[b, :, pl.ds(0, w)], local.at[p, 1]),
            pltpu.make_async_copy(w_down.at[at, :], down_w.at[b, pl.ds(0, w), :], local.at[p, 2]),
        ]
        for c in copies:
            c.start()
        loads.append(copies)

    load(0)
    load(1)
    for p in range(5):
        at, w, b = tile(p), 512 if p < 4 else 384, p % 2
        for c in loads[p]:
            c.wait()
        wg, wu, wd = gate_w.at[b, :, pl.ds(0, w)], up_w.at[b, :, pl.ds(0, w)], down_w.at[b, pl.ds(0, w), :]
        gate = mm(normed[...], wg[...])
        up = mm(normed[...], wu[...])
        back = mm_t(gy[...], wd[...])
        sig = 1.0 / (1.0 + jnp.exp(-gate))
        silu = gate * sig
        hid[:, at] = (silu * up).astype(BF)
        gu[:, at] = (back * silu).astype(BF)
        gg[:, at] = (back * up * sig * (1.0 + gate * (1.0 - sig))).astype(BF)
        mlp = mm(hid[:, at], wd[...])
        grad = mm_t(gg[:, at], wg[...]) + mm_t(gu[:, at], wu[...])
        if p == 0:
            mlp_total[...] = mlp
            gn_total[...] = grad
        elif p < 4:
            mlp_total[...] += mlp
            gn_total[...] += grad
        else:
            mlp_out[...] = (mlp_total[...] + mlp).astype(BF)
            gn[...] = (gn_total[...] + grad).astype(BF)
        if p + 2 < 5:
            load(p + 2)
    met(7)
    for i in range(4):
        swap.start(i)
    chains = []

    def advance(n):
        if n < 0 or n >= 15:
            return
        kind, p, c = chains[n]
        if n in MORE:
            c.finish(0, (g_more if kind == "g" else d_more).at[MORE[n]])
            return
        c.finish(0, (g0 if kind == "g" else d0).at[p])
        c.start(1, (g0 if kind == "g" else d0).at[p], (g1 if kind == "g" else d1).at[p], send.at[1, n], recv.at[1, n])

    for p in range(5):
        w = 512 if p < 4 else 384
        for j in range(3):
            n = len(chains)
            if j < 2:
                q, src = 5 * j + p, (gg, gu)[j]
                dst = g_src.at[q]
                dst[:, pl.ds(0, w)] = t_mm(normed[...], src[:, tile(p)]).astype(BF)
                if w < 512:
                    dst[:, pl.ds(w, 512 - w)] = jnp.zeros((896, 512 - w), BF)
                c = Chain(896, 512, G_KINDS, n, dp, t)
                chains.append(("g", q, c))
                c.start(0, dst, g0.at[q], send.at[0, n], recv.at[0, n])
            else:
                dst = d_src.at[p]
                dst[pl.ds(0, w), :] = t_mm(hid[:, tile(p)], gy[...]).astype(BF)
                if w < 512:
                    dst[pl.ds(w, 512 - w), :] = jnp.zeros((512 - w, 896), BF)
                c = Chain(512, 896, D_KINDS, n, dp, t)
                chains.append(("d", p, c))
                c.start(0, dst, d0.at[p], send.at[0, n], recv.at[0, n])
            advance(n - 2)
    advance(13)
    advance(14)
    for i in range(4):
        gn_out[pl.ds(i * 128, 128), :] = swap.take(i)
    for n, (kind, p, c) in enumerate(chains):
        if n not in MORE:
            c.finish(1, (g_out if kind == "g" else d_out).at[p])


def wide(*operands):
    return pl.pallas_call(
        wide_kernel,
        out_shape=(
            jax.ShapeDtypeStruct((512, 896), F32),
            jax.ShapeDtypeStruct((512, 896), BF),
            jax.ShapeDtypeStruct((10, *G_SHAPES[1]), BF),
            jax.ShapeDtypeStruct((5, *D_SHAPES[1]), BF),
            jax.ShapeDtypeStruct((3, *G_SHAPES[0]), BF),
            jax.ShapeDtypeStruct((2, *D_SHAPES[0]), BF),
        ),
        in_specs=[VMEM_SPEC] * 2 + [ANY_SPEC] * 3,
        out_specs=(VMEM_SPEC,) * 6,
        scratch_shapes=[
            pltpu.VMEM((512, 896), F32),
            pltpu.VMEM((512, 896), F32),
            pltpu.VMEM((512, 896), BF),
            pltpu.VMEM((512, 896), BF),
            pltpu.VMEM((512, 2432), BF),
            pltpu.VMEM((512, 2432), BF),
            pltpu.VMEM((512, 2432), BF),
            pltpu.VMEM((2, 896, 512), BF),
            pltpu.VMEM((2, 896, 512), BF),
            pltpu.VMEM((2, 512, 896), BF),
            pltpu.VMEM((10, 896, 512), BF),
            pltpu.VMEM((5, 512, 896), BF),
            pltpu.VMEM((10, *G_SHAPES[0]), BF),
            pltpu.VMEM((5, *D_SHAPES[0]), BF),
            pltpu.VMEM((10, *G_SHAPES[1]), BF),
            pltpu.VMEM((5, *D_SHAPES[1]), BF),
            DMA((4,)), DMA((4,)), DMA((2, 15)), DMA((2, 15)), DMA((5, 3)),
        ],
        compiler_params=params(3),
        name="wide",
    )(*operands)


class Message:
    def __init__(self, link, size):
        self.link, self.size, self.lands = link, size, None


class Plan:
    LATENCY = 2.2
    RATE = {"core": 600e3, "tn": 46e3}

    def __init__(self):
        self.tasks = []

    def add(self, act, cost, after=(), needs=(), sends=(), rank=5):
        task = dict(act=act, cost=cost, after=list(after), needs=list(needs), sends=list(sends), rank=rank, done=False)
        self.tasks.append(task)
        return task

    def run(self):
        now, free = 0.0, {}
        left = list(self.tasks)
        while left:
            open_ = [x for x in left if all(y["done"] for y in x["after"]) and all(m.lands is not None for m in x["needs"])]
            at = {id(x): max([now] + [m.lands for m in x["needs"]]) for x in open_}
            ready = [x for x in open_ if at[id(x)] <= now]
            task = min(ready, key=lambda x: x["rank"]) if ready else min(open_, key=lambda x: at[id(x)])
            now = at[id(task)] + task["cost"]
            task["act"]()
            task["done"] = True
            left.remove(task)
            for m in task["sends"]:
                links = LINKS if m.link == "all" else (m.link,)
                for link in links:
                    begin = max(now, free.get(link, 0.0))
                    free[link] = begin + m.size / len(links) / self.RATE.get(link, 46e3)
                m.lands = max(free[link] for link in links) + self.LATENCY
        return now


def finish_kernel(
    lengths, g_in, d_in, g_more, d_more, normed, q_in, k_in, v_in, lse, mixed, mlp, residual, gn2, gy, stream,
    wq, wk, wv, wo, vecs, table, squares,
    gate_o, up_o, down_o, query_o, kv_o, out_o, small_o, res_o, gtok_o,
    mlp_got, gn, gn_got, sides, mask, ga, gm, gq, gk_t, gv_t, grad_res,
    q_src, o_src, k_src, small_buf, small_got,
    g1, d1, g2, g3, g4, g5, d2, d3, d4, d5, q0, q1, q2, q3, q4, q5, o0, o1, o2, o3, o4, o5, k0, k1, k2, k3, k4, k5,
    x_send, x_recv, send, recv, s_send, s_recv,
    r_buf, r_mid0, r_mid1, r_send, r_recv, t_buf, t_mid0, t_mid1, t_send, t_recv,
):
    dp, t = coords()
    spot = (dp // 8 + t * (1 - 2 * (dp // 8 % 2)), dp % 8)
    length = lengths[group_of(dp, t)]
    swap_gn = Swap(gn, gn_got, x_send.at[0], x_recv.at[0], dp, t)
    swap_mlp = Swap(mlp, mlp_got, x_send.at[1], x_recv.at[1], dp, t)
    mail_res = Mail(r_buf, (r_mid0, r_mid1), res_o, spot, r_send, r_recv, dp, t)
    mail_tok = Mail(t_buf, (t_mid0, t_mid1), gtok_o, spot, t_send, t_recv, dp, t)
    across = (partner("x", *partner("core", dp, t)))
    greet(neighbours(dp, t) + [swap_gn.who, across])
    plan = Plan()
    qg, og, kg = (q0, q1, q2, q3, q4, q5), (o0, o1, o2, o3, o4, o5), (k0, k1, k2, k3, k4, k5)
    chains = []
    for p in range(5):
        for j in range(3):
            n = len(chains)
            if j < 2:
                q = 5 * j + p
                c = Chain(896, 512, G_KINDS, n, dp, t)
                bufs = [g_more.at[MORE[n]], g1.at[MORE[n]]] if n in MORE else [None, g_in.at[q]]
                c.bufs = bufs + [r.at[q] for r in (g2, g3, g4, g5)]
                c.full, c.base = (gate_o, up_o)[j], (0, 512 * p)
            else:
                c = Chain(512, 896, D_KINDS, n, dp, t)
                bufs = [d_more.at[MORE[n]], d1.at[MORE[n]]] if n in MORE else [None, d_in.at[p]]
                c.bufs = bufs + [r.at[p] for r in (d2, d3, d4, d5)]
                c.full, c.base = down_o, (512 * p, 0)
            c.n = n
            chains.append(c)
    late = []
    for i, (c, bufs, full) in enumerate((
        (Chain(512, 896, D_KINDS, 0, dp, t), qg, query_o),
        (Chain(512, 896, D_KINDS, 2, dp, t), og, out_o),
        (Chain(128, 896, K_KINDS, 4, dp, t), kg, kv_o),
    )):
        c.n, c.bufs, c.full, c.base = 15 + i, list(bufs), full, (0, 0)
        late.append(c)

    def follow(c, s, src, begin, rank):
        def go(s, src=None):
            c.start(s, c.bufs[s - 1] if src is None else src, c.bufs[s], send.at[c.n, s], recv.at[c.n, s])

        def back(s):
            c.gather_start(s, c.full, c.base, send.at[c.n, 6 + s], recv.at[c.n, 6 + s])

        def size(s):
            return 2.0 * c.shapes[s + 1][0] * c.shapes[s + 1][1]

        message = Message(c.dims[s], size(s))
        task = plan.add(functools.partial(go, s, src), 0.1, begin, sends=[message], rank=rank)
        for k in range(s, 6):
            def step(k=k):
                c.finish(k, c.bufs[k])
                if k < 5:
                    go(k + 1)
                else:
                    c.spot(6, c.full, c.base)[...] = c.bufs[5][...]
                    back(c.last)

            after = Message(c.dims[k + 1], size(k + 1)) if k < 5 else Message(c.dims[c.last], size(c.last))
            task = plan.add(step, 0.1 + size(k) / 2e6, [task], [message], [after], rank)
            message = after
        for k in range(c.last, -1, -1):
            def step(k=k):
                c.gather_finish()
                if k > 0:
                    back(k - 1)

            after = Message(c.dims[k - 1], size(k - 1))
            task = plan.add(step, 0.1, [task], [message], [after] if k > 0 else [], rank)
            message = after

    meeting = plan.add(lambda: met(16), 0.5, rank=9)
    for c in chains:
        first = 1 if c.n in MORE else 2
        follow(c, first, None, [meeting], 4)
    swapped = [Message("tn", 128 * 896 * 2.0) for _ in range(4)]
    sent = plan.add(lambda: [swap_mlp.start(j) for j in range(4)], 0.2, [meeting], sends=swapped, rank=3)

    def norm_two(i):
        at = pl.ds(i * 128, 128)
        res, grad = residual[at, :], gn2[at, :]
        inverse = lax.rsqrt(jnp.mean(res * res, axis=-1, keepdims=True) + epsilon)
        unit = res * inverse
        total = jnp.sum((grad * unit).reshape(16, 8, 896), axis=0)
        scaled = grad * vecs[1:2, :]
        mean = jnp.mean(scaled * unit, axis=-1, keepdims=True)
        final = gy[at, :].astype(F32) + inverse * (scaled - unit * mean)
        grad_res[at, :] = final
        ga[at, :] = final.astype(BF)
        if i == 0:
            small_buf[0] = jnp.zeros((8, 896), F32)
        small_buf[0, 1:2, :] += jnp.sum(total, axis=0, keepdims=True)

    normed_back = [plan.add(functools.partial(norm_two, i), 0.6, rank=5) for i in range(4)]

    def prepare():
        fill_mask(mask, length)
        for side in range(2):
            sides[side] = one_head(k_in[...], side)
            sides[2 + side] = one_head(v_in[...], side)
        gk_t[...] = jnp.zeros((64, 512), F32)
        gv_t[...] = jnp.zeros((64, 512), F32)

    prepared = plan.add(prepare, 0.6, rank=5)

    def out_back():
        gm[:, pl.ds(384, 128)] = jnp.zeros((512, 128), BF)
        gm[:, pl.ds(0, 448)] = mm_t(ga[...], wo[...]).astype(BF)

    mixed_back = plan.add(out_back, 0.8, normed_back, rank=5)

    def heads(b, p):
        rows, keys = pl.ds(256 * b, 256), pl.ds(0, 256 * (b + 1))
        lanes = pl.ds(128 * p, 128)
        cos, sin = spread(table[rows, :])
        pair, pair_gm = q_in[rows, lanes], gm[rows, lanes]
        pair_t, pair_gm_t = pair.T, pair_gm.T
        grad = jnp.zeros((256, 128), F32)
        for side in range(2 if p < 3 else 1):
            h = 2 * p + side
            score = mm_t(pair, sides[side, keys, :]) + mask[rows, keys]
            probs = jnp.exp(score - lse[rows, h : h + 1])
            grad_probs = mm_t(pair_gm, sides[2 + side, keys, :])
            inner = jnp.sum(probs * grad_probs, axis=-1, keepdims=True)
            grad_scores = (probs * (grad_probs - inner)).astype(BF)
            grad = grad + mm(grad_scores, sides[side, keys, :])
            half = slice(64 * side, 64 * side + 64)
            gk_t[:, keys] += mm(pair_t[half, :], grad_scores)
            gv_t[:, keys] += mm(pair_gm_t[half, :], probs.astype(BF))
        gq[rows, lanes] = turn(grad, cos, -sin).astype(BF)

    key_grads = [None, None]

    def norm_part(b):
        rows = pl.ds(256 * b, 256)
        flat = table[rows, :].T
        cos_t, sin_t = flat[0:32], flat[64:96]
        one, two = gk_t[0:32, rows] * 0.125, gk_t[32:64, rows] * 0.125
        whole = jnp.concatenate([one * cos_t + two * sin_t, two * cos_t - one * sin_t, gv_t[:, rows]], axis=0).astype(BF)
        gkv = whole.T
        key_grads[b] = (whole, jnp.sum(gkv.astype(F32), axis=0, keepdims=True))
        part = mm(gq[rows, pl.ds(0, 448)], wq[...]) + mm(gkv[:, 0:64], wk[...]) + mm(gkv[:, 64:128], wv[...])
        gn[rows, :] = part.astype(BF)
        swap_gn.start(2 * b)
        swap_gn.start(2 * b + 1)

    returned = [Message("tn", 128 * 896 * 2.0) for _ in range(4)]
    before, parts = [prepared, mixed_back], [None, None]
    for b in (1, 0):
        before = [plan.add(functools.partial(heads, b, p), (1.0 + b) * (1.0 if p < 3 else 0.5), before, rank=5) for p in range(4)][-1:]
        parts[b] = plan.add(functools.partial(norm_part, b), 1.0, before + [meeting], sends=returned[2 * b : 2 * b + 2], rank=5)
        before = [parts[b]]

    def make_kv():
        whole = jnp.concatenate([key_grads[0][0], key_grads[1][0]], axis=1)
        k_src[...] = mm(whole, normed[...]).astype(BF)
        small_buf[0, 2:3, 0:448] = jnp.sum(gq[:, pl.ds(0, 448)].astype(F32), axis=0, keepdims=True)
        small_buf[0, 2:3, 512:640] = key_grads[0][1] + key_grads[1][1]
        small_buf[0, 3:4, :] = jnp.sum(squares[...], axis=0, keepdims=True)

    def make_q():
        q_src[...] = t_mm(gq[...], normed[...]).astype(BF)

    def make_o():
        o_src[...] = t_mm(mixed[...], ga[...]).astype(BF)

    made_q = plan.add(make_q, 0.8, [parts[0]], rank=5)
    made_kv = plan.add(make_kv, 0.6, [parts[0]], rank=5)
    made_o = plan.add(make_o, 0.8, [mixed_back], rank=6)
    follow(late[0], 0, q_src, [made_q, meeting], 2)
    follow(late[2], 0, k_src, [made_kv, meeting], 2)
    follow(late[1], 0, o_src, [made_o, meeting], 2)

    def output(i):
        at = pl.ds(i * 128, 128)
        valid = lax.broadcasted_iota(jnp.int32, (128, 896), 0) + i * 128 < length
        branch = jnp.where(valid, swap_mlp.take(i), 0.0)
        result = jnp.where(valid, residual[at, :] + branch, 0.0)
        r_buf[pl.ds(i * 2, 2)] = result.reshape(2, 8, 8, 896).astype(BF)
        for row, x in ((4, result), (5, branch)):
            some = jnp.sum((x * x).reshape(16, 8, 896), axis=0)
            small_buf[0, row : row + 1, :] += jnp.sum(some, axis=0, keepdims=True)

    outputs = [plan.add(functools.partial(output, i), 0.5, [sent] + normed_back, swapped[i : i + 1], rank=6) for i in range(4)]

    def post(mail, ready, rank):
        one, two = Message("all", 2 * 458752.0), Message("all", 2 * 458752.0)
        a = plan.add(mail.first, 0.8, ready, sends=[one], rank=rank)
        b = plan.add(mail.second, 0.9, [a], [one], [two], rank)
        plan.add(mail.last, 0.2, [b], [two], rank=rank)

    post(mail_res, outputs + [meeting], 6)

    def norm_one(i):
        at = pl.ds(i * 128, 128)
        grad = swap_gn.take(i)
        row = stream[at, :].astype(F32)
        inverse = lax.rsqrt(jnp.mean(row * row, axis=-1, keepdims=True) + epsilon)
        unit = row * inverse
        total = jnp.sum((grad * unit).reshape(16, 8, 896), axis=0)
        scaled = grad * vecs[0:1, :]
        mean = jnp.mean(scaled * unit, axis=-1, keepdims=True)
        final = grad_res[at, :] + inverse * (scaled - unit * mean)
        t_buf[pl.ds(i * 2, 2)] = final.reshape(2, 8, 8, 896).astype(BF)
        small_buf[0, 0:1, :] += jnp.sum(total, axis=0, keepdims=True)

    finals = [plan.add(functools.partial(norm_one, i), 0.6, [parts[i // 2]], returned[i : i + 1], rank=1) for i in range(4)]
    post(mail_tok, finals, 0)

    def quartet(s):
        if s == 0:
            return [partner("core", dp, t), partner("x", dp, t), across]
        one, two = ("ya", "yb") if s == 1 else ("za", "zb")
        return [partner(one, dp, t), partner(two, dp, t), partner(one, *partner(two, dp, t))]

    posted = {}

    def share(s):
        posted[s] = [
            remote(small_buf.at[s], small_got.at[3 * s + i], s_send.at[3 * s + i], s_recv.at[3 * s + i], who)
            for i, who in enumerate(quartet(s))
        ]
        for c in posted[s]:
            c.start()

    def collect(s):
        for c in posted[s]:
            c.wait()
        small_buf[s + 1] = (small_buf[s] + small_got[3 * s]) + (small_got[3 * s + 1] + small_got[3 * s + 2])
        if s < 2:
            share(s + 1)
        else:
            small_o[...] = small_buf[3]

    message = Message("x", 28672.0)
    task = plan.add(functools.partial(share, 0), 0.2, finals + outputs + [made_kv], sends=[message], rank=1)
    for s in range(3):
        after = Message(("ya", "za", "za")[s], 28672.0)
        task = plan.add(functools.partial(collect, s), 0.2, [task], [message], [after] if s < 2 else [], rank=1)
        message = after
    plan.run()


def finish(*operands):
    return pl.pallas_call(
        finish_kernel,
        out_shape=(
            jax.ShapeDtypeStruct((896, 2560), BF),
            jax.ShapeDtypeStruct((896, 2560), BF),
            jax.ShapeDtypeStruct((2560, 896), BF),
            jax.ShapeDtypeStruct((512, 896), BF),
            jax.ShapeDtypeStruct((128, 896), BF),
            jax.ShapeDtypeStruct((512, 896), BF),
            jax.ShapeDtypeStruct((8, 896), F32),
            MAIL,
            MAIL,
        ),
        in_specs=[SMEM_SPEC] + [VMEM_SPEC] * 22,
        out_specs=(VMEM_SPEC,) * 9,
        scratch_shapes=[
            pltpu.VMEM((512, 896), BF),
            pltpu.VMEM((512, 896), BF),
            pltpu.VMEM((512, 896), BF),
            pltpu.VMEM((4, 512, 128), BF),
            pltpu.VMEM((512, 512), F32),
            pltpu.VMEM((512, 896), BF),
            pltpu.VMEM((512, 512), BF),
            pltpu.VMEM((512, 512), BF),
            pltpu.VMEM((64, 512), F32),
            pltpu.VMEM((64, 512), F32),
            pltpu.VMEM((512, 896), F32),
            pltpu.VMEM((512, 896), BF),
            pltpu.VMEM((512, 896), BF),
            pltpu.VMEM((128, 896), BF),
            pltpu.VMEM((4, 8, 896), F32),
            pltpu.VMEM((9, 8, 896), F32),
            pltpu.VMEM((3, *G_SHAPES[1]), BF),
            pltpu.VMEM((2, *D_SHAPES[1]), BF),
            *[pltpu.VMEM((10, *s), BF) for s in G_SHAPES[2:]],
            *[pltpu.VMEM((5, *s), BF) for s in D_SHAPES[2:]],
            *[pltpu.VMEM(s, BF) for s in D_SHAPES],
            *[pltpu.VMEM(s, BF) for s in D_SHAPES],
            *[pltpu.VMEM(s, BF) for s in K_SHAPES],
            DMA((2, 4)), DMA((2, 4)), DMA((18, 12)), DMA((18, 12)), DMA((9,)), DMA((9,)), *MAIL_SCRATCH, *MAIL_SCRATCH,
        ],
        compiler_params=params(4),
        name="finish",
    )(*operands)


def unpack_kernel(
    order, lengths, gate, up, down, query, kv, out_w, small, res, gtok,
    gate_o, up_o, down_o, query_o, key_o, value_o, out_o, res_o, gtok_o, small_o,
    where_from,
):
    i = pl.program_id(0)

    @pl.when(i == 0)
    def _():
        def note(g, carry):
            where_from[order[g]] = g
            return carry + lengths[g]

        count = lax.fori_loop(0, 64, note, 0).astype(F32) * 896.0
        sums = jnp.sum(small[...], axis=-1, keepdims=True)
        small_o[...] = small[...]
        small_o[3:6, 0:128] = jnp.broadcast_to(jnp.sqrt(sums[3:6] / count), (3, 128))

    rows = pl.ds(pl.multiple_of(i * 64, 64), 64)
    gate_o[...] = gate[rows, pl.ds(0, 2432)].astype(F32)
    up_o[...] = up[rows, pl.ds(0, 2432)].astype(F32)
    down_o[...] = down[pl.ds(pl.multiple_of(i * 176, 16), 176), :].astype(F32)

    @pl.when(i < 7)
    def _():
        query_o[...] = query[rows, :].astype(F32)
        out_o[...] = out_w[rows, :].astype(F32)

    @pl.when(i == 0)
    def _():
        key_o[...] = kv[pl.ds(0, 64), :].astype(F32)
        value_o[...] = kv[pl.ds(64, 64), :].astype(F32)

    @pl.when(i < 8)
    def _():
        for j in range(8):
            slot = where_from[jnp.minimum(i, 7) * 8 + j]
            res_o[j] = res[slot]
            gtok_o[j] = gtok[slot]


def unpack(*operands):
    return pl.pallas_call(
        unpack_kernel,
        grid=(14,),
        out_shape=(
            jax.ShapeDtypeStruct((896, 2432), F32),
            jax.ShapeDtypeStruct((896, 2432), F32),
            jax.ShapeDtypeStruct((2432, 896), F32),
            jax.ShapeDtypeStruct((448, 896), F32),
            jax.ShapeDtypeStruct((64, 896), F32),
            jax.ShapeDtypeStruct((64, 896), F32),
            jax.ShapeDtypeStruct((448, 896), F32),
            BLOCK,
            BLOCK,
            jax.ShapeDtypeStruct((8, 896), F32),
        ),
        in_specs=[SMEM_SPEC] * 2 + [VMEM_SPEC] * 9,
        out_specs=(
            pl.BlockSpec((64, 2432), lambda i: (i, 0)),
            pl.BlockSpec((64, 2432), lambda i: (i, 0)),
            pl.BlockSpec((176, 896), lambda i: (i, 0)),
            pl.BlockSpec((64, 896), lambda i: (jnp.minimum(i, 6), 0)),
            pl.BlockSpec((64, 896), lambda i: (0, 0)),
            pl.BlockSpec((64, 896), lambda i: (0, 0)),
            pl.BlockSpec((64, 896), lambda i: (jnp.minimum(i, 6), 0)),
            pl.BlockSpec((8, 8, 896), lambda i: (jnp.minimum(i, 7), 0, 0)),
            pl.BlockSpec((8, 8, 896), lambda i: (jnp.minimum(i, 7), 0, 0)),
            pl.BlockSpec((8, 896), lambda i: (0, 0)),
        ),
        scratch_shapes=[pltpu.SMEM((64,), jnp.int32)],
        compiler_params=pltpu.CompilerParams(vmem_limit_bytes=VMEM_LIMIT),
        name="unpack",
    )(*operands)


def on_device(
    tokens,
    cotangent,
    lengths,
    deal_order,
    gain_attn,
    w_query,
    b_query,
    w_key,
    b_key,
    w_value,
    b_value,
    w_out,
    gain_mlp,
    w_gate,
    w_up,
    w_down,
):
    table = jnp.asarray(rope_table())
    biases = jnp.concatenate([b_query, b_key, b_value, jnp.zeros((320,), BF)])
    blank = jnp.zeros((896,), BF)
    vecs = jnp.stack([gain_attn, gain_mlp, biases] + [blank] * 5).astype(F32)
    stream = dispatch(deal_order, tokens).reshape(512, 896)
    normed, q, k, v, lse, mixed, residual, normed_two, gy, squares = meet(
        deal_order, lengths, stream, cotangent, w_query.T, w_key.T, w_value.T, w_out, vecs, table
    )
    gn2, mlp, g_part, d_part, g_more, d_more = wide(normed_two, gy, w_gate, w_up, w_down)
    gate, up, down, query, kv, out_w, small, sent_res, sent_tok = finish(
        lengths, g_part, d_part, g_more, d_more, normed, q, k, v, lse, mixed, mlp, residual, gn2, gy, stream,
        w_query.T, w_key.T, w_value.T, w_out, vecs, table, squares,
    )
    gate, up, down, query, key, value, out_w, layer_out, grad_tokens, small = unpack(
        deal_order, lengths, gate, up, down, query, kv, out_w, small,
        sent_res.reshape(64, 8, 896), sent_tok.reshape(64, 8, 896),
    )
    rms_values = jnp.stack([small[4, 0], small[3, 0], small[5, 0]])
    return (
        layer_out,
        grad_tokens,
        small[0],
        query.T,
        small[2, :448],
        key.T,
        small[2, 512:576],
        value.T,
        small[2, 576:640],
        out_w,
        small[1],
        gate,
        up,
        down,
        rms_values,
    )


def solution(mesh):
    in_specs = (
        P(None, "dp", None),
        P(None, "dp", None),
        P(),
        P(),
        P(),
        P(None, "tensor"),
        P("tensor"),
        P(None, "tensor"),
        P("tensor"),
        P(None, "tensor"),
        P("tensor"),
        P("tensor", None),
        P(),
        P(None, "tensor"),
        P(None, "tensor"),
        P("tensor", None),
    )
    out_specs = (
        P(None, "dp", None),
        P(None, "dp", None),
        P(),
        P(None, "tensor"),
        P("tensor"),
        P(None, "tensor"),
        P("tensor"),
        P(None, "tensor"),
        P("tensor"),
        P("tensor", None),
        P(),
        P(None, "tensor"),
        P(None, "tensor"),
        P("tensor", None),
        P(),
    )
    return jax.shard_map(
        on_device, mesh=mesh, in_specs=in_specs, out_specs=out_specs, check_vma=False
    )
```

profile of v0, /device:TPU:1, one launch (start us, length us, event | category | flops | bytes accessed | tf_op | source)
XLA Modules:
  0.0 258.0 jit_solution(8305509312628379152)
XLA Ops:
  0.7 0.8 pad_maximum_fusion
  1.5 0.7 stack.18
  2.1 0.7 stack.19
  2.9 0.6 convert_element_type.3.vecs
  3.5 25.6 %dispatch.1 = bf16[8,8,8,896]{3,2,1,0:T(8,128)(2,1)} custom-call(s32[64]{0:T(128)} %order.5, bf16[64,8,896]{2,1,0:T(8,128)(2,1)} %tok.1), custom_call_target="tpu_custom_call" | custom-call | tf_op jit(solution)/shard_map/dispatch/pallas_call | solution.py:257
  29.1 34.3 %meet.1 = (bf16[512,896]{1,0:T(8,128)(2,1)}, bf16[512,512]{1,0:T(8,128)(2,1)}, bf16[512,128]{1,0:T(8,128)(2,1)}, bf16[512,128]{1,0:T(8,128)(2,1)}, f32[512,128]{...) custom-call(s32[64]{0:T(128)} %order.5, ...), custom_call_target="tpu_custom_call" | custom-call | tf_op jit(solution)/shard_map/meet/pallas_call | solution.py:421
  63.4 47.0 %wide.1 = (f32[512,896]{1,0:T(8,128)}, bf16[512,896]{1,0:T(8,128)(2,1)}, bf16[10,896,128]{2,1,0:T(8,128)(2,1)}, bf16[5,128,896]{2,1,0:T(8,128)(2,1)}, bf16[3,896...) custom-call(bf16[512,896]{1,0:T(8,128)(2,1)} %get-tuple-element.50.normed, bf16[512,896]{1,0:T(8,128)(2,1)} %get-tuple-element.51.gy, ...), custom_call_target="tpu_custom_call" | custom-call | tf_op jit(solution)/shard_map/wide/pallas_call | solution.py:546
  110.5 121.2 %finish.1 = (bf16[896,2560]{1,0:T(8,128)(2,1)}, bf16[896,2560]{1,0:T(8,128)(2,1)}, bf16[2560,896]{1,0:T(8,128)(2,1)}, bf16[512,896]{1,0:T(8,128)(2,1)}, bf16[128...) custom-call(s32[64]{0:T(128)} %lengths.5, ...), custom_call_target="tpu_custom_call" | custom-call | tf_op jit(solution)/shard_map/finish/pallas_call | solution.py:874
  231.7 18.3 %unpack.1 = (f32[896,2432]{1,0:T(8,128)}, f32[896,2432]{1,0:T(8,128)}, f32[2432,896]{1,0:T(8,128)}, f32[448,896]{1,0:T(8,128)}, f32[64,896]{1,0:T(8,128)}, /*ind...) custom-call(s32[64]{0:T(128)} %order.5, ...), custom_call_target="tpu_custom_call" | custom-call | tf_op jit(solution)/shard_map/unpack/pallas_call | solution.py:962
  249.9 1.3 slice_bitcast_fusion
  251.3 1.3 fusion
  252.6 2.5 pad_maximum_fusion.1
  255.1 1.3 slice.25
  256.4 1.4 slice_reduce_fusion
  (5 shorter events, 0.1 us)
where the time goes:
time: 262 us; the launch traced here: 258 us
  Pallas kernels  246 us (94%)
  local copies, waits for them, and re-layouts  6.82 us (3%)
  other arithmetic  3.93 us (2%)
    pallas_call x1, Pallas kernels, finish(): pl.pallas_call(finish_kernel, out_shape=(jax.ShapeDtypeStruct((896, 2560)...  121 us
    pallas_call x1, Pallas kernels, wide(): pl.pallas_call(wide_kernel, out_shape=(jax.ShapeDtypeStruct((512, 896), F...  47 us
    pallas_call x1, Pallas kernels, meet(): pl.pallas_call(meet_kernel, out_shape=(rows, wide_rows, pair, pair, jax.S...  34.3 us
    pallas_call x1, Pallas kernels, dispatch(): pl.pallas_call(dispatch_kernel, out_shape=MAIL, in_specs=[SMEM_SPEC, VMEM...  25.6 us
    pallas_call x1, Pallas kernels, unpack(): pl.pallas_call(unpack_kernel, grid=(14,), out_shape=(jax.ShapeDtypeStruct...  18.3 us

commit v1 on v0

--- a/solution.py
+++ b/solution.py
@@ -174,8 +174,8 @@
 DMA = pltpu.SemaphoreType.DMA
 
 
-def params(cid):
-    return pltpu.CompilerParams(collective_id=cid, has_side_effects=True, vmem_limit_bytes=VMEM_LIMIT)
+def params(cid, limit=VMEM_LIMIT):
+    return pltpu.CompilerParams(collective_id=cid, has_side_effects=True, vmem_limit_bytes=limit)
 
 
 class Mail:
@@ -242,29 +242,6 @@
             buf[a, b] = rows[order[group_of(a * 8 + b, t)]]
 
 
-def dispatch_kernel(order, tok, out, buf, mid0, mid1, send, recv):
-    dp, t = coords()
-    greet(neighbours(dp, t))
-    sort_out(order, tok, buf, dp, t)
-    mail = Mail(buf, (mid0, mid1), out, (dp // 8, dp % 8), send, recv, dp, t)
-    met(14)
-    mail.first()
-    mail.second()
-    mail.last()
-
-
-def dispatch(order, tokens):
-    return pl.pallas_call(
-        dispatch_kernel,
-        out_shape=MAIL,
-        in_specs=[SMEM_SPEC, VMEM_SPEC],
-        out_specs=VMEM_SPEC,
-        scratch_shapes=MAIL_SCRATCH,
-        compiler_params=params(1),
-        name="dispatch",
-    )(order, tokens)
-
-
 def mm(a, b):
     return jnp.dot(a, b, preferred_element_type=F32)
 
@@ -331,23 +308,31 @@
 
 
 def meet_kernel(
-    order, lengths, stream, cot, wq, wk, wv, wo, vecs, table,
-    normed, q_o, k_o, v_o, lse_o, mixed, residual, normed_two, gy, squares,
-    sides, mask, x, got, cot_in, send, recv, buf, mid0, mid1, c_send, c_recv,
+    order, lengths, tok, cot, wq, wk, wv, wo, vecs, table,
+    normed, q_o, k_o, v_o, lse_o, mixed, residual, normed_two, gy, squares, stream,
+    sides, mask, x, got, tok_in, cot_in, send, recv, buf, mid0, mid1, c_send, c_recv, t_buf, t_mid0, t_mid1, t_send, t_recv,
 ):
     dp, t = coords()
     swap = Swap(x, got, send, recv, dp, t)
     mail = Mail(buf, (mid0, mid1), cot_in, (dp // 8, dp % 8), c_send, c_recv, dp, t)
     greet(neighbours(dp, t) + [swap.who])
     length = lengths[group_of(dp, t)]
+    sort_out(order, tok, t_buf, dp, t)
+    tokens = Mail(t_buf, (t_mid0, t_mid1), tok_in, (dp // 8, dp % 8), t_send, t_recv, dp, t)
+    met(15)
+    tokens.first()
     sort_out(order, cot, buf, dp, t)
+    fill_mask(mask, length)
+    cos, sin = spread(table[...])
+    tokens.second()
+    tokens.last()
+    mail.first()
     for i in range(4):
         at = pl.ds(i * 128, 128)
-        row = stream[at, :].astype(F32)
+        row = tok_in[pl.ds(i * 2, 2)].astype(F32).reshape(128, 896)
+        stream[at, :] = row.astype(BF)
         inverse = lax.rsqrt(jnp.mean(row * row, axis=-1, keepdims=True) + epsilon)
         normed[at, :] = (row * inverse * vecs[0:1, :]).astype(BF)
-    fill_mask(mask, length)
-    cos, sin = spread(table[...])
     k = mm_t(normed[...], wk[...]) + vecs[2:3, 448:512]
     v = mm_t(normed[...], wv[...]) + vecs[2:3, 512:576]
     k2 = turn(jnp.concatenate([k, k], axis=1), cos, sin)
@@ -356,8 +341,6 @@
     for side in range(2):
         sides[side] = one_head(k_o[...], side)
         sides[2 + side] = one_head(v_o[...], side)
-    met(15)
-    mail.first()
     for p in range(4):
         w = 128 if p < 3 else 64
         lanes = pl.ds(128 * p, w)
@@ -422,43 +405,145 @@
         meet_kernel,
         out_shape=(
             rows, wide_rows, pair, pair, jax.ShapeDtypeStruct((512, 128), F32), wide_rows,
-            jax.ShapeDtypeStruct((512, 896), F32), rows, rows, jax.ShapeDtypeStruct((8, 896), F32),
+            jax.ShapeDtypeStruct((512, 896), F32), rows, rows, jax.ShapeDtypeStruct((8, 896), F32), rows,
         ),
         in_specs=[SMEM_SPEC] * 2 + [VMEM_SPEC] * 8,
-        out_specs=(VMEM_SPEC,) * 10,
+        out_specs=(VMEM_SPEC,) * 11,
         scratch_shapes=[
             pltpu.VMEM((4, 512, 128), BF),
             pltpu.VMEM((512, 512), F32),
             pltpu.VMEM((512, 896), BF),
             pltpu.VMEM((512, 896), BF),
             pltpu.VMEM((8, 8, 8, 896), BF),
-            DMA((4,)), DMA((4,)), *MAIL_SCRATCH,
+            pltpu.VMEM((8, 8, 8, 896), BF),
+            DMA((4,)), DMA((4,)), *MAIL_SCRATCH, *MAIL_SCRATCH,
         ],
         compiler_params=params(2),
         name="meet",
     )(*operands)
 
 
-MORE = {10: 0, 11: 0, 12: 1, 13: 2, 14: 1}
+class Message:
+    def __init__(self, link, size):
+        self.link, self.size, self.lands = link, size, None
+
+
+class Plan:
+    LATENCY = 2.2
+    RATE = {"core": 600e3, "tn": 46e3}
+
+    def __init__(self):
+        self.tasks = []
+
+    def add(self, act, cost, after=(), needs=(), sends=(), rank=5):
+        task = dict(act=act, cost=cost, after=list(after), needs=list(needs), sends=list(sends), rank=rank, done=False)
+        self.tasks.append(task)
+        return task
+
+    def run(self):
+        now, free = 0.0, {}
+        left = list(self.tasks)
+        while left:
+            open_ = [x for x in left if all(y["done"] for y in x["after"]) and all(m.lands is not None for m in x["needs"])]
+            at = {id(x): max([now] + [m.lands for m in x["needs"]]) for x in open_}
+            ready = [x for x in open_ if at[id(x)] <= now]
+            task = min(ready, key=lambda x: x["rank"]) if ready else min(open_, key=lambda x: at[id(x)])
+            now = at[id(task)] + task["cost"]
+            task["act"]()
+            task["done"] = True
+            left.remove(task)
+            for m in task["sends"]:
+                links = LINKS if m.link == "all" else (m.link,)
+                for link in links:
+                    begin = max(now, free.get(link, 0.0))
+                    free[link] = begin + m.size / len(links) / self.RATE.get(link, 46e3)
+                m.lands = max(free[link] for link in links) + self.LATENCY
+        return now
+
+
+def follow(plan, c, first, last, begin, rank, up=False):
+    def go(s):
+        c.start(s, c.bufs[s - 1], c.gots[s], c.send.at[s], c.recv.at[s])
+
+    def back(s):
+        c.gather_start(s, c.full, c.base, c.send.at[6 + s], c.recv.at[6 + s])
+
+    def size(s):
+        return 2.0 * c.shapes[s + 1][0] * c.shapes[s + 1][1]
+
+    if first > last and not up:
+        return begin
+    message = Message(c.dims[first], size(first))
+    task = plan.add(functools.partial(go, first), 0.1, begin, sends=[message], rank=rank)
+    for k in range(first, last + 1):
+        def step(k=k):
+            c.finish(k, c.bufs[k])
+            if k < last:
+                go(k + 1)
+            elif up:
+                c.spot(6, c.full, c.base)[...] = c.bufs[5][...]
+                back(c.last)
+
+        after = None
+        if k < last:
+            after = Message(c.dims[k + 1], size(k + 1))
+        elif up:
+            after = Message(c.dims[c.last], size(c.last))
+        task = plan.add(step, 0.1 + size(k) / 2e6, [task], [message], [after] if after else [], rank)
+        message = after
+    if not up:
+        return [task]
+    for k in range(c.last, -1, -1):
+        def step(k=k):
+            c.gather_finish()
+            if k > 0:
+                back(k - 1)
+
+        after = Message(c.dims[k - 1], size(k - 1)) if k > 0 else None
+        task = plan.add(step, 0.1, [task], [message], [after] if after else [], rank)
+        message = after
+    return [task]
+
+
+EARLY = 2
+STAGE = [4, 4, 4, 4, 4, 4, 2, 2, 2, 3, 2, 1, 1, 1, 1]
+
+
+def kind_of(n):
+    p, j = n // 3, n % 3
+    return (p, j, 896, 512, G_KINDS) if j < 2 else (p, j, 512, 896, D_KINDS)
+
+
+def stage_shape(n, s):
+    _, _, rows, lanes, kinds = kind_of(n)
+    return ([(rows, lanes)] + halves(rows, lanes, kinds))[s + 1]
 
 
 def tile(p):
     return pl.ds(512 * p, 512 if p < 4 else 384)
 
 
-def wide_kernel(
-    normed, gy, w_gate, w_up, w_down, gn_out, mlp_out, g_out, d_out, g_more, d_more,
-    gn_total, mlp_total, gn, got, hid, gg, gu, gate_w, up_w, down_w, g_src, d_src, g0, d0, g1, d1,
-    x_send, x_recv, send, recv, local,
-):
+def wide_kernel(*refs):
+    normed, gy, w_gate, w_up, w_down, gn_out, mlp_out = refs[:7]
+    parts, refs = refs[7:22], refs[22:]
+    gn_total, mlp_total, gn, got, hid, gg, gu, gate_w, up_w, down_w, x_send, x_recv, send, recv, local = refs[:15]
+    refs = list(refs[15:])
     dp, t = coords()
     swap = Swap(gn, got, x_send, x_recv, dp, t)
     greet([swap.who] + [partner(d, dp, t) for d in ("core",) + LINKS])
+    chains = []
+    for n in range(15):
+        p, j, rows, lanes, kinds = kind_of(n)
+        c = Chain(rows, lanes, kinds, n, dp, t)
+        c.source = refs.pop(0)
+        c.gots = [refs.pop(0) for _ in range(STAGE[n] + 1)]
+        c.bufs = c.gots[:-1] + [parts[n]] + [c.source]
+        c.send, c.recv = send.at[n], recv.at[n]
+        chains.append(c)
     loads = []
 
     def load(p):
-        at, w = tile(p), 512 if p < 4 else 384
-        b = p % 2
+        at, w, b = tile(p), 512 if p < 4 else 384, p % 2
         copies = [
             pltpu.make_async_copy(w_gate.at[:, at], gate_w.at[b, :, pl.ds(0, w)], local.at[p, 0]),
             pltpu.make_async_copy(w_up.at[:, at], up_w.at[b, :, pl.ds(0, w)], local.at[p, 1]),
@@ -468,9 +553,7 @@
             c.start()
         loads.append(copies)
 
-    load(0)
-    load(1)
-    for p in range(5):
+    def layer(p):
         at, w, b = tile(p), 512 if p < 4 else 384, p % 2
         for c in loads[p]:
             c.wait()
@@ -496,65 +579,60 @@
             gn[...] = (gn_total[...] + grad).astype(BF)
         if p + 2 < 5:
             load(p + 2)
-    met(7)
+
+    def weight(n):
+        p, j = n // 3, n % 3
+        w, dst = 512 if p < 4 else 384, chains[n].source
+        if j < 2:
+            dst[:, pl.ds(0, w)] = t_mm(normed[...], (gg, gu)[j][:, tile(p)]).astype(BF)
+            if w < 512:
+                dst[:, pl.ds(w, 512 - w)] = jnp.zeros((896, 512 - w), BF)
+        else:
+            dst[pl.ds(0, w), :] = t_mm(hid[:, tile(p)], gy[...]).astype(BF)
+            if w < 512:
+                dst[pl.ds(w, 512 - w), :] = jnp.zeros((512 - w, 896), BF)
+
+    load(0)
+    load(1)
+    plan = Plan()
+    meeting = plan.add(lambda: met(7), 0.3, rank=6)
+    layers, done = [], []
+    for p in range(5):
+        layers.append(plan.add(functools.partial(layer, p), 3.4 if p < 4 else 2.6, layers[-1:], rank=5))
+        if p == 0:
+            layers.append(meeting)
+            meeting["after"] = layers[:1]
+        if p < EARLY:
+            layers += [plan.add(functools.partial(weight, 3 * p + j), 0.55, layers[-1:], rank=4) for j in range(3)]
+            done += layers[-3:]
+    returned = [Message("tn", 128 * 896 * 2.0) for _ in range(4)]
+    sent = plan.add(lambda: [swap.start(i) for i in range(4)], 0.2, layers[-1:] + [meeting], sends=returned, rank=0)
+    for n in range(3 * EARLY, 15):
+        done.append(plan.add(functools.partial(weight, n), 0.55 if n < 12 else 0.4, [sent], rank=5))
+    for n, c in enumerate(chains):
+        follow(plan, c, 0, STAGE[n], [done[n], meeting], 2)
+
+    def take(i):
+        gn_out[pl.ds(i * 128, 128), :] = swap.take(i)
+
     for i in range(4):
-        swap.start(i)
-    chains = []
-
-    def advance(n):
-        if n < 0 or n >= 15:
-            return
-        kind, p, c = chains[n]
-        if n in MORE:
-            c.finish(0, (g_more if kind == "g" else d_more).at[MORE[n]])
-            return
-        c.finish(0, (g0 if kind == "g" else d0).at[p])
-        c.start(1, (g0 if kind == "g" else d0).at[p], (g1 if kind == "g" else d1).at[p], send.at[1, n], recv.at[1, n])
-
-    for p in range(5):
-        w = 512 if p < 4 else 384
-        for j in range(3):
-            n = len(chains)
-            if j < 2:
-                q, src = 5 * j + p, (gg, gu)[j]
-                dst = g_src.at[q]
-                dst[:, pl.ds(0, w)] = t_mm(normed[...], src[:, tile(p)]).astype(BF)
-                if w < 512:
-                    dst[:, pl.ds(w, 512 - w)] = jnp.zeros((896, 512 - w), BF)
-                c = Chain(896, 512, G_KINDS, n, dp, t)
-                chains.append(("g", q, c))
-                c.start(0, dst, g0.at[q], send.at[0, n], recv.at[0, n])
-            else:
-                dst = d_src.at[p]
-                dst[pl.ds(0, w), :] = t_mm(hid[:, tile(p)], gy[...]).astype(BF)
-                if w < 512:
-                    dst[pl.ds(w, 512 - w), :] = jnp.zeros((512 - w, 896), BF)
-                c = Chain(512, 896, D_KINDS, n, dp, t)
-                chains.append(("d", p, c))
-                c.start(0, dst, d0.at[p], send.at[0, n], recv.at[0, n])
-            advance(n - 2)
-    advance(13)
-    advance(14)
-    for i in range(4):
-        gn_out[pl.ds(i * 128, 128), :] = swap.take(i)
-    for n, (kind, p, c) in enumerate(chains):
-        if n not in MORE:
-            c.finish(1, (g_out if kind == "g" else d_out).at[p])
+        plan.add(functools.partial(take, i), 0.2, [sent], returned[i : i + 1], rank=3)
+    plan.run()
 
 
 def wide(*operands):
+    room = []
+    for n in range(15):
+        room += [pltpu.VMEM(stage_shape(n, s), BF) for s in range(-1, STAGE[n] + 1)]
     return pl.pallas_call(
         wide_kernel,
         out_shape=(
             jax.ShapeDtypeStruct((512, 896), F32),
             jax.ShapeDtypeStruct((512, 896), BF),
-            jax.ShapeDtypeStruct((10, *G_SHAPES[1]), BF),
-            jax.ShapeDtypeStruct((5, *D_SHAPES[1]), BF),
-            jax.ShapeDtypeStruct((3, *G_SHAPES[0]), BF),
-            jax.ShapeDtypeStruct((2, *D_SHAPES[0]), BF),
+            *[jax.ShapeDtypeStruct(stage_shape(n, STAGE[n]), BF) for n in range(15)],
         ),
         in_specs=[VMEM_SPEC] * 2 + [ANY_SPEC] * 3,
-        out_specs=(VMEM_SPEC,) * 6,
+        out_specs=(VMEM_SPEC,) * 17,
         scratch_shapes=[
             pltpu.VMEM((512, 896), F32),
             pltpu.VMEM((512, 896), F32),
@@ -566,67 +644,27 @@
             pltpu.VMEM((2, 896, 512), BF),
             pltpu.VMEM((2, 896, 512), BF),
             pltpu.VMEM((2, 512, 896), BF),
-            pltpu.VMEM((10, 896, 512), BF),
-            pltpu.VMEM((5, 512, 896), BF),
-            pltpu.VMEM((10, *G_SHAPES[0]), BF),
-            pltpu.VMEM((5, *D_SHAPES[0]), BF),
-            pltpu.VMEM((10, *G_SHAPES[1]), BF),
-            pltpu.VMEM((5, *D_SHAPES[1]), BF),
-            DMA((4,)), DMA((4,)), DMA((2, 15)), DMA((2, 15)), DMA((5, 3)),
+            DMA((4,)), DMA((4,)), DMA((15, 12)), DMA((15, 12)), DMA((5, 3)),
+            *room,
         ],
         compiler_params=params(3),
         name="wide",
     )(*operands)
 
 
-class Message:
-    def __init__(self, link, size):
-        self.link, self.size, self.lands = link, size, None
-
-
-class Plan:
-    LATENCY = 2.2
-    RATE = {"core": 600e3, "tn": 46e3}
-
-    def __init__(self):
-        self.tasks = []
-
-    def add(self, act, cost, after=(), needs=(), sends=(), rank=5):
-        task = dict(act=act, cost=cost, after=list(after), needs=list(needs), sends=list(sends), rank=rank, done=False)
-        self.tasks.append(task)
-        return task
-
-    def run(self):
-        now, free = 0.0, {}
-        left = list(self.tasks)
-        while left:
-            open_ = [x for x in left if all(y["done"] for y in x["after"]) and all(m.lands is not None for m in x["needs"])]
-            at = {id(x): max([now] + [m.lands for m in x["needs"]]) for x in open_}
-            ready = [x for x in open_ if at[id(x)] <= now]
-            task = min(ready, key=lambda x: x["rank"]) if ready else min(open_, key=lambda x: at[id(x)])
-            now = at[id(task)] + task["cost"]
-            task["act"]()
-            task["done"] = True
-            left.remove(task)
-            for m in task["sends"]:
-                links = LINKS if m.link == "all" else (m.link,)
-                for link in links:
-                    begin = max(now, free.get(link, 0.0))
-                    free[link] = begin + m.size / len(links) / self.RATE.get(link, 46e3)
-                m.lands = max(free[link] for link in links) + self.LATENCY
-        return now
-
-
-def finish_kernel(
-    lengths, g_in, d_in, g_more, d_more, normed, q_in, k_in, v_in, lse, mixed, mlp, residual, gn2, gy, stream,
-    wq, wk, wv, wo, vecs, table, squares,
-    gate_o, up_o, down_o, query_o, kv_o, out_o, small_o, res_o, gtok_o,
-    mlp_got, gn, gn_got, sides, mask, ga, gm, gq, gk_t, gv_t, grad_res,
-    q_src, o_src, k_src, small_buf, small_got,
-    g1, d1, g2, g3, g4, g5, d2, d3, d4, d5, q0, q1, q2, q3, q4, q5, o0, o1, o2, o3, o4, o5, k0, k1, k2, k3, k4, k5,
-    x_send, x_recv, send, recv, s_send, s_recv,
-    r_buf, r_mid0, r_mid1, r_send, r_recv, t_buf, t_mid0, t_mid1, t_send, t_recv,
-):
+LATE_TURN = [0, 1, 2, 3, 4, 0, 1, 2, 3]
+
+
+def finish_kernel(*refs):
+    lengths, parts_in, refs = refs[0], refs[1:16], refs[16:]
+    (normed, q_in, k_in, v_in, lse, mixed, mlp, residual, gn2, gy, stream,
+     wq, wk, wv, wo, vecs, table, squares) = refs[:18]
+    gate_f, up_f, down_f, query_f, kv_f, out_f, small_o, res_o, gtok_o = refs[18:27]
+    (mlp_got, gn, gn_got, sides, mask, ga, gm, gq, gk_t, gv_t, grad_res,
+     small_buf, small_got) = refs[27:40]
+    x_send, x_recv, send, recv, s_send, s_recv = refs[40:46]
+    r_buf, r_mid0, r_mid1, r_send, r_recv, t_buf, t_mid0, t_mid1, t_send, t_recv = refs[46:56]
+    refs = list(refs[56:])
     dp, t = coords()
     spot = (dp // 8 + t * (1 - 2 * (dp // 8 % 2)), dp % 8)
     length = lengths[group_of(dp, t)]
@@ -637,71 +675,33 @@
     across = (partner("x", *partner("core", dp, t)))
     greet(neighbours(dp, t) + [swap_gn.who, across])
     plan = Plan()
-    qg, og, kg = (q0, q1, q2, q3, q4, q5), (o0, o1, o2, o3, o4, o5), (k0, k1, k2, k3, k4, k5)
     chains = []
-    for p in range(5):
-        for j in range(3):
-            n = len(chains)
-            if j < 2:
-                q = 5 * j + p
-                c = Chain(896, 512, G_KINDS, n, dp, t)
-                bufs = [g_more.at[MORE[n]], g1.at[MORE[n]]] if n in MORE else [None, g_in.at[q]]
-                c.bufs = bufs + [r.at[q] for r in (g2, g3, g4, g5)]
-                c.full, c.base = (gate_o, up_o)[j], (0, 512 * p)
-            else:
-                c = Chain(512, 896, D_KINDS, n, dp, t)
-                bufs = [d_more.at[MORE[n]], d1.at[MORE[n]]] if n in MORE else [None, d_in.at[p]]
-                c.bufs = bufs + [r.at[p] for r in (d2, d3, d4, d5)]
-                c.full, c.base = down_o, (512 * p, 0)
-            c.n = n
-            chains.append(c)
-    late = []
-    for i, (c, bufs, full) in enumerate((
-        (Chain(512, 896, D_KINDS, 0, dp, t), qg, query_o),
-        (Chain(512, 896, D_KINDS, 2, dp, t), og, out_o),
-        (Chain(128, 896, K_KINDS, 4, dp, t), kg, kv_o),
-    )):
-        c.n, c.bufs, c.full, c.base = 15 + i, list(bufs), full, (0, 0)
+    for n in range(15):
+        p, j, rows, lanes, kinds = kind_of(n)
+        c = Chain(rows, lanes, kinds, n, dp, t)
+        c.gots = [None] * (STAGE[n] + 1) + [refs.pop(0) for _ in range(STAGE[n] + 1, 6)]
+        c.bufs = list(c.gots)
+        c.bufs[STAGE[n]] = parts_in[n]
+        c.send, c.recv = send.at[n], recv.at[n]
+        c.full, c.base = (gate_f, up_f, down_f)[j], (0, 512 * p) if j < 2 else (512 * p, 0)
+        chains.append(c)
+    late, late_whole = [], []
+    for i in range(9):
+        c = Chain(128, 896, K_KINDS, LATE_TURN[i], dp, t)
+        if i % 4 == 0:
+            whole = refs.pop(0)
+        c.source = whole.at[pl.ds(128 * (i % 4), 128), :] if i < 8 else whole
+        c.gots = [refs.pop(0) for _ in range(6)]
+        c.bufs = c.gots + [c.source]
+        c.send, c.recv = send.at[15 + i], recv.at[15 + i]
+        c.full, c.base = (query_f, out_f, kv_f)[i // 4], (128 * (i % 4), 0)
         late.append(c)
-
-    def follow(c, s, src, begin, rank):
-        def go(s, src=None):
-            c.start(s, c.bufs[s - 1] if src is None else src, c.bufs[s], send.at[c.n, s], recv.at[c.n, s])
-
-        def back(s):
-            c.gather_start(s, c.full, c.base, send.at[c.n, 6 + s], recv.at[c.n, 6 + s])
-
-        def size(s):
-            return 2.0 * c.shapes[s + 1][0] * c.shapes[s + 1][1]
-
-        message = Message(c.dims[s], size(s))
-        task = plan.add(functools.partial(go, s, src), 0.1, begin, sends=[message], rank=rank)
-        for k in range(s, 6):
-            def step(k=k):
-                c.finish(k, c.bufs[k])
-                if k < 5:
-                    go(k + 1)
-                else:
-                    c.spot(6, c.full, c.base)[...] = c.bufs[5][...]
-                    back(c.last)
-
-            after = Message(c.dims[k + 1], size(k + 1)) if k < 5 else Message(c.dims[c.last], size(c.last))
-            task = plan.add(step, 0.1 + size(k) / 2e6, [task], [message], [after], rank)
-            message = after
-        for k in range(c.last, -1, -1):
-            def step(k=k):
-                c.gather_finish()
-                if k > 0:
-                    back(k - 1)
-
-            after = Message(c.dims[k - 1], size(k - 1))
-            task = plan.add(step, 0.1, [task], [message], [after] if k > 0 else [], rank)
-            message = after
-
-    meeting = plan.add(lambda: met(16), 0.5, rank=9)
-    for c in chains:
-        first = 1 if c.n in MORE else 2
-        follow(c, first, None, [meeting], 4)
+        if i % 4 == 0:
+            late_whole.append(whole)
+    q_src, o_src, k_src = late_whole
+    meeting = plan.add(lambda: met(16), 0.5, rank=0)
+    for n, c in enumerate(chains):
+        follow(plan, c, STAGE[n] + 1, 5, [meeting], 4, True)
     swapped = [Message("tn", 128 * 896 * 2.0) for _ in range(4)]
     sent = plan.add(lambda: [swap_mlp.start(j) for j in range(4)], 0.2, [meeting], sends=swapped, rank=3)
 
@@ -721,6 +721,7 @@
         small_buf[0, 1:2, :] += jnp.sum(total, axis=0, keepdims=True)
 
     normed_back = [plan.add(functools.partial(norm_two, i), 0.6, rank=5) for i in range(4)]
+    meeting["after"] = normed_back[:1]
 
     def prepare():
         fill_mask(mask, length)
@@ -795,10 +796,9 @@
 
     made_q = plan.add(make_q, 0.8, [parts[0]], rank=5)
     made_kv = plan.add(make_kv, 0.6, [parts[0]], rank=5)
-    made_o = plan.add(make_o, 0.8, [mixed_back], rank=6)
-    follow(late[0], 0, q_src, [made_q, meeting], 2)
-    follow(late[2], 0, k_src, [made_kv, meeting], 2)
-    follow(late[1], 0, o_src, [made_o, meeting], 2)
+    made_o = plan.add(make_o, 0.8, [mixed_back], rank=4.5)
+    for i, c in enumerate(late):
+        follow(plan, c, 0, 5, [(made_q, made_o, made_kv)[i // 4], meeting], 2, True)
 
     def output(i):
         at = pl.ds(i * 128, 128)
@@ -871,20 +871,26 @@
 
 
 def finish(*operands):
+    wide_out = pltpu.VMEM((896, 2560), BF), pltpu.VMEM((896, 2560), BF), pltpu.VMEM((2560, 896), BF)
+    room = []
+    for n in range(15):
+        room += [pltpu.VMEM(stage_shape(n, s), BF) for s in range(STAGE[n] + 1, 6)]
+    for i in range(9):
+        if i % 4 == 0:
+            room.append(pltpu.VMEM((512 if i < 8 else 128, 896), BF))
+        room += [pltpu.VMEM(x, BF) for x in K_SHAPES]
     return pl.pallas_call(
         finish_kernel,
         out_shape=(
-            jax.ShapeDtypeStruct((896, 2560), BF),
-            jax.ShapeDtypeStruct((896, 2560), BF),
-            jax.ShapeDtypeStruct((2560, 896), BF),
-            jax.ShapeDtypeStruct((512, 896), BF),
-            jax.ShapeDtypeStruct((128, 896), BF),
-            jax.ShapeDtypeStruct((512, 896), BF),
-            jax.ShapeDtypeStruct((8, 896), F32),
-            MAIL,
-            MAIL,
+            *wide_out,
+            pltpu.VMEM((512, 896), BF),
+            pltpu.VMEM((128, 896), BF),
+            pltpu.VMEM((512, 896), BF),
+            pltpu.VMEM((8, 896), F32),
+            pltpu.VMEM((8, 8, 8, 896), BF),
+            pltpu.VMEM((8, 8, 8, 896), BF),
         ),
-        in_specs=[SMEM_SPEC] + [VMEM_SPEC] * 22,
+        in_specs=[SMEM_SPEC] + [VMEM_SPEC] * 33,
         out_specs=(VMEM_SPEC,) * 9,
         scratch_shapes=[
             pltpu.VMEM((512, 896), BF),
@@ -898,28 +904,19 @@
             pltpu.VMEM((64, 512), F32),
             pltpu.VMEM((64, 512), F32),
             pltpu.VMEM((512, 896), F32),
-            pltpu.VMEM((512, 896), BF),
-            pltpu.VMEM((512, 896), BF),
-            pltpu.VMEM((128, 896), BF),
             pltpu.VMEM((4, 8, 896), F32),
             pltpu.VMEM((9, 8, 896), F32),
-            pltpu.VMEM((3, *G_SHAPES[1]), BF),
-            pltpu.VMEM((2, *D_SHAPES[1]), BF),
-            *[pltpu.VMEM((10, *s), BF) for s in G_SHAPES[2:]],
-            *[pltpu.VMEM((5, *s), BF) for s in D_SHAPES[2:]],
-            *[pltpu.VMEM(s, BF) for s in D_SHAPES],
-            *[pltpu.VMEM(s, BF) for s in D_SHAPES],
-            *[pltpu.VMEM(s, BF) for s in K_SHAPES],
-            DMA((2, 4)), DMA((2, 4)), DMA((18, 12)), DMA((18, 12)), DMA((9,)), DMA((9,)), *MAIL_SCRATCH, *MAIL_SCRATCH,
+            DMA((2, 4)), DMA((2, 4)), DMA((24, 12)), DMA((24, 12)), DMA((9,)), DMA((9,)),
+            *MAIL_SCRATCH, *MAIL_SCRATCH, *room,
         ],
-        compiler_params=params(4),
+        compiler_params=params(4, 45 << 20),
         name="finish",
     )(*operands)
 
 
 def unpack_kernel(
     order, lengths, gate, up, down, query, kv, out_w, small, res, gtok,
-    gate_o, up_o, down_o, query_o, key_o, value_o, out_o, res_o, gtok_o, small_o,
+    gate_o, up_o, down_o, query_o, key_o, value_o, out_o, res_o, gtok_o, gain1_o, gain2_o, bq_o, bk_o, bv_o, rms_o,
     where_from,
 ):
     i = pl.program_id(0)
@@ -931,9 +928,18 @@
             return carry + lengths[g]
 
         count = lax.fori_loop(0, 64, note, 0).astype(F32) * 896.0
-        sums = jnp.sum(small[...], axis=-1, keepdims=True)
-        small_o[...] = small[...]
-        small_o[3:6, 0:128] = jnp.broadcast_to(jnp.sqrt(sums[3:6] / count), (3, 128))
+        rms = jnp.sqrt(jnp.sum(small[...], axis=-1, keepdims=True) / count)
+        lane = lax.broadcasted_iota(jnp.int32, (1, 128), 1)
+        line = jnp.where(lane == 0, rms[4:5], jnp.where(lane == 1, rms[3:4], rms[5:6]))
+        gain1_o[...] = small[0, :]
+        gain2_o[...] = small[1, :]
+        bq_o[...] = small[2, 0:448]
+        pair = small[2:3, 512:640]
+        bk_o[...] = pair[0, 0:64]
+        bv_o[...] = pltpu.roll(pair, 64, 1)[0, 0:64]
+        rms_o[...] = line[0, 0:3]
+        key_o[...] = kv[pl.ds(0, 64), :].astype(F32)
+        value_o[...] = kv[pl.ds(64, 64), :].astype(F32)
 
     rows = pl.ds(pl.multiple_of(i * 64, 64), 64)
     gate_o[...] = gate[rows, pl.ds(0, 2432)].astype(F32)
@@ -944,11 +950,6 @@
     def _():
         query_o[...] = query[rows, :].astype(F32)
         out_o[...] = out_w[rows, :].astype(F32)
-
-    @pl.when(i == 0)
-    def _():
-        key_o[...] = kv[pl.ds(0, 64), :].astype(F32)
-        value_o[...] = kv[pl.ds(64, 64), :].astype(F32)
 
     @pl.when(i < 8)
     def _():
@@ -959,6 +960,8 @@
 
 
 def unpack(*operands):
+    rows = lambda i: (i, 0)
+    some = lambda i: (jnp.minimum(i, 6), 0)
     return pl.pallas_call(
         unpack_kernel,
         grid=(14,),
@@ -972,25 +975,25 @@
             jax.ShapeDtypeStruct((448, 896), F32),
             BLOCK,
             BLOCK,
-            jax.ShapeDtypeStruct((8, 896), F32),
+            *[jax.ShapeDtypeStruct((n,), F32) for n in (896, 896, 448, 64, 64, 3)],
         ),
         in_specs=[SMEM_SPEC] * 2 + [VMEM_SPEC] * 9,
         out_specs=(
-            pl.BlockSpec((64, 2432), lambda i: (i, 0)),
-            pl.BlockSpec((64, 2432), lambda i: (i, 0)),
-            pl.BlockSpec((176, 896), lambda i: (i, 0)),
-            pl.BlockSpec((64, 896), lambda i: (jnp.minimum(i, 6), 0)),
+            pl.BlockSpec((64, 2432), rows),
+            pl.BlockSpec((64, 2432), rows),
+            pl.BlockSpec((176, 896), rows),
+            pl.BlockSpec((64, 896), some),
             pl.BlockSpec((64, 896), lambda i: (0, 0)),
             pl.BlockSpec((64, 896), lambda i: (0, 0)),
-            pl.BlockSpec((64, 896), lambda i: (jnp.minimum(i, 6), 0)),
+            pl.BlockSpec((64, 896), some),
             pl.BlockSpec((8, 8, 896), lambda i: (jnp.minimum(i, 7), 0, 0)),
             pl.BlockSpec((8, 8, 896), lambda i: (jnp.minimum(i, 7), 0, 0)),
-            pl.BlockSpec((8, 896), lambda i: (0, 0)),
+            *[VMEM_SPEC] * 6,
         ),
         scratch_shapes=[pltpu.SMEM((64,), jnp.int32)],
-        compiler_params=pltpu.CompilerParams(vmem_limit_bytes=VMEM_LIMIT),
+        compiler_params=pltpu.CompilerParams(vmem_limit_bytes=16 << 20),
         name="unpack",
-    )(*operands)
+    )(*operands[:2], *[pltpu.with_memory_space_constraint(x, pltpu.VMEM) for x in operands[2:]])
 
 
 def on_device(
@@ -1015,32 +1018,33 @@
     biases = jnp.concatenate([b_query, b_key, b_value, jnp.zeros((320,), BF)])
     blank = jnp.zeros((896,), BF)
     vecs = jnp.stack([gain_attn, gain_mlp, biases] + [blank] * 5).astype(F32)
-    stream = dispatch(deal_order, tokens).reshape(512, 896)
-    normed, q, k, v, lse, mixed, residual, normed_two, gy, squares = meet(
-        deal_order, lengths, stream, cotangent, w_query.T, w_key.T, w_value.T, w_out, vecs, table
+    normed, q, k, v, lse, mixed, residual, normed_two, gy, squares, stream = meet(
+        deal_order, lengths, tokens, cotangent, w_query.T, w_key.T, w_value.T, w_out, vecs, table
     )
-    gn2, mlp, g_part, d_part, g_more, d_more = wide(normed_two, gy, w_gate, w_up, w_down)
+    gn2, mlp, *sums = wide(normed_two, gy, w_gate, w_up, w_down)
     gate, up, down, query, kv, out_w, small, sent_res, sent_tok = finish(
-        lengths, g_part, d_part, g_more, d_more, normed, q, k, v, lse, mixed, mlp, residual, gn2, gy, stream,
+        lengths, *sums, normed, q, k, v, lse, mixed, mlp, residual, gn2, gy, stream,
         w_query.T, w_key.T, w_value.T, w_out, vecs, table, squares,
     )
-    gate, up, down, query, key, value, out_w, layer_out, grad_tokens, small = unpack(
+    (
+        gate, up, down, query, key, value, out_w, layer_out, grad_tokens,
+        gain_one, gain_two, bias_query, bias_key, bias_value, rms_values,
+    ) = unpack(
         deal_order, lengths, gate, up, down, query, kv, out_w, small,
         sent_res.reshape(64, 8, 896), sent_tok.reshape(64, 8, 896),
     )
-    rms_values = jnp.stack([small[4, 0], small[3, 0], small[5, 0]])
     return (
         layer_out,
         grad_tokens,
-        small[0],
+        gain_one,
         query.T,
-        small[2, :448],
+        bias_query,
         key.T,
-        small[2, 512:576],
+        bias_key,
         value.T,
-        small[2, 576:640],
+        bias_value,
         out_w,
-        small[1],
+        gain_two,
         gate,
         up,
         down,

time: 262 us -> 232 us (0.89)
  Pallas kernels: 246 us -> 225 us
  local copies, waits for them, and re-layouts: 6.82 us -> 1.45 us
    pallas_call x2 -> x1, Pallas kernels: 147 us -> 101 us  [finish(): pl.pallas_call(finish_kernel, out_shape=(*wide_out, pltpu.VMEM((512, 896)...]
    pallas_call x1, Pallas kernels: 34.3 us -> 57.3 us  [meet(): pl.pallas_call(meet_kernel, out_shape=(rows, wide_rows, pair, pair, jax.S...]
    pallas_call x1, Pallas kernels: 47 us -> 53.9 us  [wide(): pl.pallas_call(wide_kernel, out_shape=(jax.ShapeDtypeStruct((512, 896), F...]
    pallas_call x1, Pallas kernels: 18.3 us -> 12.7 us  [unpack(): pl.pallas_call(unpack_kernel, grid=(14,), out_shape=(jax.ShapeDtypeStruct...]
    slice x3 -> x0, local copies, waits for them, and re-layouts: 4.05 us -> none  [the longest x1 1.44 us: on_device(): small[1]]
where the time goes in v1:
time: 232 us; the launch traced here: 229 us
  Pallas kernels  225 us (97%)
    pallas_call x1, Pallas kernels, finish(): pl.pallas_call(finish_kernel, out_shape=(*wide_out, pltpu.VMEM((512, 896)...  101 us
    pallas_call x1, Pallas kernels, meet(): pl.pallas_call(meet_kernel, out_shape=(rows, wide_rows, pair, pair, jax.S...  57.3 us
    pallas_call x1, Pallas kernels, wide(): pl.pallas_call(wide_kernel, out_shape=(jax.ShapeDtypeStruct((512, 896), F...  53.9 us
    pallas_call x1, Pallas kernels, unpack(): pl.pallas_call(unpack_kernel, grid=(14,), out_shape=(jax.ShapeDtypeStruct...  12.7 us

profile of v1, /device:TPU:1, one launch (start us, length us, event | category | flops | bytes accessed | tf_op | source)
XLA Modules:
  0.0 229.2 jit_solution(10501495560225570333)
XLA Ops:
  0.7 0.8 pad_maximum_fusion
  1.5 0.7 stack.15
  2.1 0.7 stack.16
  2.9 0.6 convert_element_type.3.vecs.refs_31_
  3.5 57.3 %meet.1 = (bf16[512,896]{1,0:T(8,128)(2,1)}, bf16[512,512]{1,0:T(8,128)(2,1)}, bf16[512,128]{1,0:T(8,128)(2,1)}, bf16[512,128]{1,0:T(8,128)(2,1)}, f32[512,128]{...) custom-call(s32[64]{0:T(128)} %order.3, ...), custom_call_target="tpu_custom_call" | custom-call | tf_op jit(solution)/shard_map/meet/pallas_call | solution.py:404
  60.8 53.9 %wide.1 = (f32[512,896]{1,0:T(8,128)}, bf16[512,896]{1,0:T(8,128)(2,1)}, bf16[112,128]{1,0:T(8,128)(2,1)}, bf16[112,128]{1,0:T(8,128)(2,1)}, bf16[16,896]{1,0:T(...) custom-call(bf16[512,896]{1,0:T(8,128)(2,1)} %get-tuple-element.67.r, ...), custom_call_target="tpu_custom_call" | custom-call | tf_op jit(solution)/shard_map/wide/pallas_call | solution.py:627
  114.7 0.0 copy-start
  114.7 0.0 copy-start.1
  114.7 101.4 %finish.1 = (bf16[896,2560]{1,0:T(8,128)(2,1)S(1)}, bf16[896,2560]{1,0:T(8,128)(2,1)S(1)}, bf16[2560,896]{1,0:T(8,128)(2,1)S(1)}, bf16[512,896]{1,0:T(8,128)(2,1...) custom-call(s32[64]{0:T(128)} %lengths.3, ...), custom_call_target="tpu_custom_call" | custom-call | tf_op jit(solution)/shard_map/finish/pallas_call | solution.py:882
  216.2 0.0 copy-done
  216.2 0.0 copy-done.1
  216.2 12.7 %unpack.1 = (f32[896,2432]{1,0:T(8,128)}, f32[896,2432]{1,0:T(8,128)}, f32[2432,896]{1,0:T(8,128)}, f32[448,896]{1,0:T(8,128)}, f32[64,896]{1,0:T(8,128)}, /*ind...) custom-call(s32[64]{0:T(128)S(1)} %copy-done.1, ...), custom_call_target="tpu_custom_call" | custom-call | tf_op jit(solution)/shard_map/unpack/pallas_call | solution.py:965
  (5 shorter events, 0.1 us)
Async XLA Ops:
  114.7 101.5 %copy-start = (s32[64]{0:T(128)S(1)}, s32[64]{0:T(128)}, u32[]{:S(2)}) copy-start(s32[64]{0:T(128)} %lengths.3) | copy-start | bytes 772
  114.7 101.5 %copy-start.1 = (s32[64]{0:T(128)S(1)}, s32[64]{0:T(128)}, u32[]{:S(2)}) copy-start(s32[64]{0:T(128)} %order.3) | copy-start | bytes 772

commit v2 on v1

--- a/solution.py
+++ b/solution.py
@@ -429,8 +429,8 @@
 
 
 class Plan:
-    LATENCY = 2.2
-    RATE = {"core": 600e3, "tn": 46e3}
+    LATENCY = 3.2
+    RATE = {"core": 500e3, "tn": 43e3}
 
     def __init__(self):
         self.tasks = []
@@ -456,7 +456,7 @@
                 links = LINKS if m.link == "all" else (m.link,)
                 for link in links:
                     begin = max(now, free.get(link, 0.0))
-                    free[link] = begin + m.size / len(links) / self.RATE.get(link, 46e3)
+                    free[link] = begin + m.size / len(links) / self.RATE.get(link, 40e3)
                 m.lands = max(free[link] for link in links) + self.LATENCY
         return now
 
@@ -505,8 +505,11 @@
     return [task]
 
 
-EARLY = 2
-STAGE = [4, 4, 4, 4, 4, 4, 2, 2, 2, 3, 2, 1, 1, 1, 1]
+EARLY = 3
+STAGE = [4, 4, 3, 4, 4, 4, 4, 3, 2, 2, 2, 1, 1, 1, 1]
+
+
+TURN = [2, 4, 1, 3, 0, 0, 1, 2, 3, 4, 0, 3, 4, 2, 1]
 
 
 def kind_of(n):
@@ -534,7 +537,7 @@
     chains = []
     for n in range(15):
         p, j, rows, lanes, kinds = kind_of(n)
-        c = Chain(rows, lanes, kinds, n, dp, t)
+        c = Chain(rows, lanes, kinds, TURN[n], dp, t)
         c.source = refs.pop(0)
         c.gots = [refs.pop(0) for _ in range(STAGE[n] + 1)]
         c.bufs = c.gots[:-1] + [parts[n]] + [c.source]
@@ -627,9 +630,9 @@
     return pl.pallas_call(
         wide_kernel,
         out_shape=(
-            jax.ShapeDtypeStruct((512, 896), F32),
-            jax.ShapeDtypeStruct((512, 896), BF),
-            *[jax.ShapeDtypeStruct(stage_shape(n, STAGE[n]), BF) for n in range(15)],
+            pltpu.VMEM((512, 896), F32),
+            pltpu.VMEM((512, 896), BF),
+            *[pltpu.VMEM(stage_shape(n, STAGE[n]), BF) for n in range(15)],
         ),
         in_specs=[VMEM_SPEC] * 2 + [ANY_SPEC] * 3,
         out_specs=(VMEM_SPEC,) * 17,
@@ -647,12 +650,22 @@
             DMA((4,)), DMA((4,)), DMA((15, 12)), DMA((15, 12)), DMA((5, 3)),
             *room,
         ],
-        compiler_params=params(3),
+        compiler_params=params(3, 52 << 20),
         name="wide",
     )(*operands)
 
 
-LATE_TURN = [0, 1, 2, 3, 4, 0, 1, 2, 3]
+FROM_WIDE = set(range(1, 16)) | {22, 24}
+
+
+def in_vmem(x):
+    return pltpu.with_memory_space_constraint(x, pltpu.VMEM)
+
+
+LATE_TURN = [2, 2, 0, 2, 2, 3, 3, 0, 3]
+RANK = [4.4, 4, 4, 4, 4, 5.5, 4.2, 4, 4.4, 4.6, 4.4, 4.2, 4.4, 4.4, 4.6]
+LATE_RANK = [2, 1, 3, 2, 4.5, 4.5, 4.5, 1, 3]
+MAIL_RANK = [3, 0]
 
 
 def finish_kernel(*refs):
@@ -678,7 +691,7 @@
     chains = []
     for n in range(15):
         p, j, rows, lanes, kinds = kind_of(n)
-        c = Chain(rows, lanes, kinds, n, dp, t)
+        c = Chain(rows, lanes, kinds, TURN[n], dp, t)
         c.gots = [None] * (STAGE[n] + 1) + [refs.pop(0) for _ in range(STAGE[n] + 1, 6)]
         c.bufs = list(c.gots)
         c.bufs[STAGE[n]] = parts_in[n]
@@ -701,7 +714,7 @@
     q_src, o_src, k_src = late_whole
     meeting = plan.add(lambda: met(16), 0.5, rank=0)
     for n, c in enumerate(chains):
-        follow(plan, c, STAGE[n] + 1, 5, [meeting], 4, True)
+        follow(plan, c, STAGE[n] + 1, 5, [meeting], RANK[n], True)
     swapped = [Message("tn", 128 * 896 * 2.0) for _ in range(4)]
     sent = plan.add(lambda: [swap_mlp.start(j) for j in range(4)], 0.2, [meeting], sends=swapped, rank=3)
 
@@ -798,7 +811,7 @@
     made_kv = plan.add(make_kv, 0.6, [parts[0]], rank=5)
     made_o = plan.add(make_o, 0.8, [mixed_back], rank=4.5)
     for i, c in enumerate(late):
-        follow(plan, c, 0, 5, [(made_q, made_o, made_kv)[i // 4], meeting], 2, True)
+        follow(plan, c, 0, 5, [(made_q, made_o, made_kv)[i // 4], meeting], LATE_RANK[i], True)
 
     def output(i):
         at = pl.ds(i * 128, 128)
@@ -818,7 +831,7 @@
         b = plan.add(mail.second, 0.9, [a], [one], [two], rank)
         plan.add(mail.last, 0.2, [b], [two], rank=rank)
 
-    post(mail_res, outputs + [meeting], 6)
+    post(mail_res, outputs + [meeting], MAIL_RANK[0])
 
     def norm_one(i):
         at = pl.ds(i * 128, 128)
@@ -834,7 +847,7 @@
         small_buf[0, 0:1, :] += jnp.sum(total, axis=0, keepdims=True)
 
     finals = [plan.add(functools.partial(norm_one, i), 0.6, [parts[i // 2]], returned[i : i + 1], rank=1) for i in range(4)]
-    post(mail_tok, finals, 0)
+    post(mail_tok, finals, MAIL_RANK[1])
 
     def quartet(s):
         if s == 0:
@@ -909,9 +922,9 @@
             DMA((2, 4)), DMA((2, 4)), DMA((24, 12)), DMA((24, 12)), DMA((9,)), DMA((9,)),
             *MAIL_SCRATCH, *MAIL_SCRATCH, *room,
         ],
-        compiler_params=params(4, 45 << 20),
+        compiler_params=params(4, 38 << 20),
         name="finish",
-    )(*operands)
+    )(*[in_vmem(x) if i in FROM_WIDE else x for i, x in enumerate(operands)])
 
 
 def unpack_kernel(

time: 232 us -> 222 us (0.957)
  Pallas kernels: 225 us -> 215 us
    pallas_call x1, Pallas kernels: 101 us -> 91.6 us  [finish(): pl.pallas_call(finish_kernel, out_shape=(*wide_out, pltpu.VMEM((512, 896)...]
where the time goes in v2:
time: 222 us; the launch traced here: 218 us
  Pallas kernels  215 us (97%)
    pallas_call x1, Pallas kernels, finish(): pl.pallas_call(finish_kernel, out_shape=(*wide_out, pltpu.VMEM((512, 896)...  91.6 us
    pallas_call x1, Pallas kernels, meet(): pl.pallas_call(meet_kernel, out_shape=(rows, wide_rows, pair, pair, jax.S...  56.9 us
    pallas_call x1, Pallas kernels, wide(): pl.pallas_call(wide_kernel, out_shape=(pltpu.VMEM((512, 896), F32), pltpu...  53.5 us
    pallas_call x1, Pallas kernels, unpack(): pl.pallas_call(unpack_kernel, grid=(14,), out_shape=(jax.ShapeDtypeStruct...  12.7 us

profile of v2, /device:TPU:1, one launch (start us, length us, event | category | flops | bytes accessed | tf_op | source)
XLA Modules:
  0.0 218.4 jit_solution(16348383037636118347)
XLA Ops:
  0.7 0.8 pad_maximum_fusion
  1.5 0.7 stack.15
  2.1 0.7 stack.16
  2.9 0.6 convert_element_type.3.vecs.refs_31_
  3.5 56.9 %meet.1 = (bf16[512,896]{1,0:T(8,128)(2,1)}, bf16[512,512]{1,0:T(8,128)(2,1)}, bf16[512,128]{1,0:T(8,128)(2,1)}, bf16[512,128]{1,0:T(8,128)(2,1)}, f32[512,128]{...) custom-call(s32[64]{0:T(128)} %order.3, ...), custom_call_target="tpu_custom_call" | custom-call | tf_op jit(solution)/shard_map/meet/pallas_call | solution.py:404
  60.4 53.5 %wide.1 = (f32[512,896]{1,0:T(8,128)S(1)}, bf16[512,896]{1,0:T(8,128)(2,1)S(1)}, bf16[112,128]{1,0:T(8,128)(2,1)S(1)}, bf16[112,128]{1,0:T(8,128)(2,1)S(1)}, bf1...) custom-call(bf16[512,896]{1,0:T(8,128)(2,1)} %get-tuple-element.67.r, ...), custom_call_target="tpu_custom_call" | custom-call | tf_op jit(solution)/shard_map/wide/pallas_call | solution.py:630
  113.9 0.0 copy-start
  113.9 0.0 copy-start.1
  113.9 91.6 %finish.1 = (bf16[896,2560]{1,0:T(8,128)(2,1)S(1)}, bf16[896,2560]{1,0:T(8,128)(2,1)S(1)}, bf16[2560,896]{1,0:T(8,128)(2,1)S(1)}, bf16[512,896]{1,0:T(8,128)(2,1...) custom-call(s32[64]{0:T(128)} %lengths.3, ...), custom_call_target="tpu_custom_call" | custom-call | tf_op jit(solution)/shard_map/finish/pallas_call | solution.py:895
  205.5 0.0 copy-done
  205.5 0.0 copy-done.1
  205.5 12.7 %unpack.1 = (f32[896,2432]{1,0:T(8,128)}, f32[896,2432]{1,0:T(8,128)}, f32[2432,896]{1,0:T(8,128)}, f32[448,896]{1,0:T(8,128)}, f32[64,896]{1,0:T(8,128)}, /*ind...) custom-call(s32[64]{0:T(128)S(1)} %copy-done.1, ...), custom_call_target="tpu_custom_call" | custom-call | tf_op jit(solution)/shard_map/unpack/pallas_call | solution.py:978
  (5 shorter events, 0.1 us)
Async XLA Ops:
  113.9 91.6 %copy-start = (s32[64]{0:T(128)S(1)}, s32[64]{0:T(128)}, u32[]{:S(2)}) copy-start(s32[64]{0:T(128)} %lengths.3) | copy-start | bytes 772
  113.9 91.6 %copy-start.1 = (s32[64]{0:T(128)S(1)}, s32[64]{0:T(128)}, u32[]{:S(2)}) copy-start(s32[64]{0:T(128)} %order.3) | copy-start | bytes 772
